TPU v7x, 256 devices: a whole 4x4x8 slice. The times are simulated.
256 devices in a mesh: tile: 16 (over z_lo, y, core), quad: 16 (over z_hi, x).
Axes of the slice: x: 4, y: 4, z: 8 (z_hi: 4, z_lo: 2; z = z_hi * 2 + z_lo), core: 2. Of those that a mesh axis runs over, the one named last changes fastest.
Arguments:
- adjoint_next: float32 [32, 32, 2048], P('quad', None, 'tile'), may hold values from -6 to 6
- saved_state: float32 [32, 32, 2048], P('quad', None, 'tile'), may hold values from 0.2 to 2
- gain_left: float32 [16, 32, 1024], P('quad'), may hold values from 0.1 to 2
- gain_right: float32 [16, 32, 1024], P('quad'), may hold values from 0.1 to 2
Outputs:
- adjoint_prev: float32 [32, 32, 2048], P('quad', None, 'tile')
All inputs are finite; a program needn't handle non-finite values.
Results may differ from a plain program's by a relative error of at most 0.0001.
Values sent between devices are 32-bit elements; how exact they have to be, the bound alone decides.
A program may use at most 64 MiB of HBM per device.

v0:
```python
import functools
import ml_dtypes
import numpy as np
import jax
import jax.numpy as jnp
from jax import lax
from jax.experimental import pallas as pl
from jax.experimental.pallas import tpu as pltpu
from jax.sharding import PartitionSpec as P

MESH = pl.DeviceIdType.MESH
NV = 32
ROOT_HALF = float(np.sqrt(0.5))


def in_real_form(matrix):
    return np.block([[matrix.real, matrix.imag], [-matrix.imag, matrix.real]])


def two_halves(matrix):
    high = matrix.astype(ml_dtypes.bfloat16)
    low = (matrix - high.astype(np.float64)).astype(ml_dtypes.bfloat16)
    return high, low


def make_tables():
    steps = np.arange(NV)
    whole = np.exp(-2j * np.pi * (steps[:, None] * steps[None, :] % NV) / NV)
    four = np.arange(4)
    quarter = np.exp(-2j * np.pi * (four[:, None] * four[None, :] % 4) / 4)
    lanes = np.kron(quarter, whole)
    slots = np.kron(np.eye(4), whole)
    blocks = [
        in_real_form(lanes),
        in_real_form(slots),
        in_real_form(np.tile(whole, (1, 4))),
        in_real_form(slots.conj() / NV),
        in_real_form(lanes.conj() / NV**2),
    ]
    rows = []
    for block in blocks:
        rows.extend(two_halves(block))
    total = in_real_form(np.tile(whole.conj() / NV, (4, 1)))
    total = np.concatenate([total, np.zeros((256, 64))], axis=1)
    rows.append(np.concatenate(two_halves(total), axis=1))
    return np.concatenate(rows, axis=0)


ROWS_OF = {
    "lanes": (0, 256, 256),
    "slots": (512, 768, 256),
    "spread": (1024, 1088, 64),
    "slots_back": (1152, 1408, 256),
    "lanes_back": (1664, 1920, 256),
}
TOTAL_ROW = 2176
TABLE_ROWS = 2432


def split(x):
    high = x.astype(jnp.bfloat16)
    low = (x - high.astype(jnp.float32)).astype(jnp.bfloat16)
    return high, low


def product(x, high, low):
    xh, xl = split(x)
    dot = functools.partial(jnp.dot, preferred_element_type=jnp.float32)
    return dot(xh, high) + dot(xl, high) + dot(xh, low)


def turned(x):
    return jnp.concatenate([x[:, :128].T, x[:, 128:].T], axis=1)


def turn_by(value, factor):
    re, im = value
    fr, fi = factor
    if abs(fi) < 1e-12 and abs(fr - 1.0) < 1e-12:
        return value
    return (re * fr - im * fi, re * fi + im * fr)


def plus(a, b):
    return (a[0] + b[0], a[1] + b[1])


def minus(a, b):
    return (a[0] - b[0], a[1] - b[1])


def four_points(x, sign):
    s0, d0 = plus(x[0], x[2]), minus(x[0], x[2])
    s1, d1 = plus(x[1], x[3]), minus(x[1], x[3])
    side = (-sign * d1[1], sign * d1[0]) if sign > 0 else (d1[1], -d1[0])
    return [plus(s0, s1), plus(d0, side), minus(s0, s1), minus(d0, side)]


def eight_points(x, sign):
    even = four_points(x[0::2], sign)
    odd = four_points(x[1::2], sign)
    o1, o2, o3 = odd[1], odd[2], odd[3]
    if sign < 0:
        o1 = ((o1[0] + o1[1]) * ROOT_HALF, (o1[1] - o1[0]) * ROOT_HALF)
        o2 = (o2[1], -o2[0])
        o3 = ((o3[1] - o3[0]) * ROOT_HALF, (o3[0] + o3[1]) * -ROOT_HALF)
    else:
        o1 = ((o1[0] - o1[1]) * ROOT_HALF, (o1[1] + o1[0]) * ROOT_HALF)
        o2 = (-o2[1], o2[0])
        o3 = ((o3[0] + o3[1]) * -ROOT_HALF, (o3[0] - o3[1]) * ROOT_HALF)
    odd = [odd[0], o1, o2, o3]
    return [plus(e, o) for e, o in zip(even, odd)] + [minus(e, o) for e, o in zip(even, odd)]


def twiddle(index, residue, sign):
    angle = sign * 2.0 * np.pi * (index * residue % NV) / NV
    return float(np.cos(angle)), float(np.sin(angle))


def forward_eight(x, residue):
    return eight_points([turn_by(v, twiddle(n, residue, -1)) for n, v in enumerate(x)], -1)


def backward_eight(x, residue):
    return [turn_by(v, twiddle(n, residue, 1)) for n, v in enumerate(eight_points(x, 1))]


def exchange_lanes(tiles):
    group = lax.broadcasted_iota(jnp.int32, (8, 128), 1) // 32
    upper = group >= 2
    odd = group % 2 == 1
    y = [None] * 4
    for h in range(2):
        y[h] = jnp.where(upper, pltpu.roll(tiles[h + 2], 64, 1), tiles[h])
        y[h + 2] = jnp.where(upper, tiles[h + 2], pltpu.roll(tiles[h], 64, 1))
    z = [None] * 4
    for h in (0, 2):
        z[h] = jnp.where(odd, pltpu.roll(y[h + 1], 32, 1), y[h])
        z[h + 1] = jnp.where(odd, y[h + 1], pltpu.roll(y[h], 96, 1))
    return z


def kernel(
    adjoint,
    state,
    gain_left,
    gain_right,
    table_hbm,
    out,
    table,
    beside,
    passed_own,
    state_sent,
    passed_sent,
    state_all,
    passed_all,
    result,
    arrived,
    gains,
    turned_gains,
    even_left,
    even_right,
    even_loss,
    spectrum,
    product_spectrum,
    work,
    loss_work,
    loss_field,
    local_sem,
    halo_sem,
    state_send,
    state_recv,
    passed_send,
    passed_recv,
    result_send,
    result_recv,
    gain_send,
    gain_recv,
    share_send,
    share_recv,
):
    tile = lax.axis_index("tile")
    quad = lax.axis_index("quad")
    tiles = lax.axis_size("tile")
    column = lax.rem(quad, 4)
    row = quad // 4
    core = lax.rem(tile, 2)
    sibling = tile + 1 - 2 * core
    ahead = quad >= 8
    up, down = lax.rem(tile + 1, tiles), lax.rem(tile + tiles - 1, tiles)
    source_tile = jnp.where(ahead, up, down)
    target_tile = jnp.where(ahead, down, up)

    fetch_table = pltpu.make_async_copy(table_hbm, table, local_sem.at[0])
    fetch_left = pltpu.make_async_copy(
        gain_left.at[0], gains.at[0, pl.ds(column * 32, 32), :], local_sem.at[1]
    )
    fetch_right = pltpu.make_async_copy(
        gain_right.at[0], gains.at[1, pl.ds(column * 32, 32), :], local_sem.at[2]
    )
    fetch_left.start()
    fetch_right.start()
    fetch_table.start()

    barrier = pltpu.get_barrier_semaphore()

    def greet(step, carry):
        peer = lax.rem(quad + step, 16)
        pl.semaphore_signal(barrier, inc=1, device_id={"quad": peer}, device_id_type=MESH)
        return carry

    lax.fori_loop(1, 16, greet, 0)
    pl.semaphore_signal(barrier, inc=1, device_id={"tile": source_tile}, device_id_type=MESH)
    pl.semaphore_signal(barrier, inc=1, device_id={"tile": sibling}, device_id_type=MESH)

    for j in range(2):
        cells = exchange_lanes([state[j, 8 * h : 8 * h + 8, :] for h in range(4)])
        for cell in range(4):
            state_sent[cell, 8 * j : 8 * j + 8, :] = cells[cell]
    state_all[pl.ds(quad * 16, 16), :] = state_sent[column]

    pl.semaphore_wait(barrier, 17)

    halo = pltpu.make_async_remote_copy(
        src_ref=adjoint,
        dst_ref=beside,
        send_sem=halo_sem.at[0],
        recv_sem=halo_sem.at[1],
        device_id={"tile": target_tile},
        device_id_type=MESH,
    )
    halo.start()

    def to_peer(sent, whole, send, recv, peer):
        return pltpu.make_async_remote_copy(
            src_ref=sent.at[lax.rem(peer, 4)],
            dst_ref=whole.at[pl.ds(quad * 16, 16), :],
            send_sem=send.at[peer],
            recv_sem=recv.at[quad],
            device_id={"quad": peer},
            device_id_type=MESH,
        )

    def from_peer(sent, whole, send, recv, peer):
        return pltpu.make_async_remote_copy(
            src_ref=sent.at[0],
            dst_ref=whole.at[pl.ds(peer * 16, 16), :],
            send_sem=send.at[peer],
            recv_sem=recv.at[peer],
            device_id={"quad": peer},
            device_id_type=MESH,
        )

    def for_peers(action):
        def body(step, carry):
            action(lax.rem(quad + step, 16))
            return carry

        lax.fori_loop(1, 16, body, 0)

    state_refs = (state_sent, state_all, state_send, state_recv)
    passed_refs = (passed_sent, passed_all, passed_send, passed_recv)
    for_peers(lambda peer: to_peer(*state_refs, peer).start())

    fetch_left.wait()
    fetch_right.wait()

    def gain_copy(position):
        return pltpu.make_async_remote_copy(
            src_ref=gains.at[core, pl.ds(column * 32, 32), :],
            dst_ref=gains.at[core, pl.ds(column * 32, 32), :],
            send_sem=gain_send.at[position],
            recv_sem=gain_recv.at[column],
            device_id={"quad": row * 4 + position},
            device_id_type=MESH,
        )

    def gain_arrival(position, kind, send, recv):
        return pltpu.make_async_remote_copy(
            src_ref=gains.at[kind, pl.ds(position * 32, 32), :],
            dst_ref=gains.at[kind, pl.ds(position * 32, 32), :],
            send_sem=send.at[position],
            recv_sem=recv.at[position],
            device_id={"tile": sibling},
            device_id_type=MESH,
        )

    for step in (1, 3, 2):
        gain_copy(lax.rem(column + step, 4)).start()

    halo.wait_recv()
    lane = lax.broadcasted_iota(jnp.int32, (8, 128), 1)
    lower = lane < 64
    odd_cell = lane // 32 % 2 == 1
    from_own = jnp.logical_xor(lower, jnp.logical_not(ahead))
    for j in range(2):
        plane = (quad * 2 + j).astype(jnp.float32)
        speed_x = jnp.abs((plane - (NV - 1) / 2.0) / NV)
        for h in range(4):
            rows = slice(8 * h, 8 * h + 8)
            own = adjoint[j, rows, :]
            second = beside[j, rows, :]
            first = jnp.where(from_own, pltpu.roll(own, 64, 1), pltpu.roll(second, 64, 1))
            partner = jnp.where(odd_cell, pltpu.roll(own, 32, 1), pltpu.roll(own, 96, 1))
            b = (lax.broadcasted_iota(jnp.int32, (8, 128), 0) + 8 * h).astype(jnp.float32)
            speed_y = jnp.abs((b - (NV - 1) / 2.0) / NV)
            passed_own[j, rows, :] = (
                own
                - speed_x * (3.0 * own - 4.0 * first + second) * 0.5
                - 2.0 * speed_y * (own - partner)
            )
        cells = exchange_lanes([passed_own[j, 8 * h : 8 * h + 8, :] for h in range(4)])
        for cell in range(4):
            passed_sent[cell, 8 * j : 8 * j + 8, :] = cells[cell]
    passed_all[pl.ds(quad * 16, 16), :] = passed_sent[column]
    for_peers(lambda peer: to_peer(*passed_refs, peer).start())

    def tables(name):
        high, low, count = ROWS_OF[name]
        return table[high : high + count, :], table[low : low + count, :]

    def one_spread(values, store, low_index):
        high, low = tables("lanes")
        mid = product(values, high[:128], low[:128])
        mid = jnp.concatenate([mid[:, :128], mid[:, 128:]], axis=0).T
        store[low_index] = product(mid, *tables("spread"))

    def plane_of(ref, low_index):
        return ref[pl.ds(low_index, 32, stride=8), :]

    fetch_table.wait()
    for_peers(lambda peer: from_peer(*state_refs, peer).wait_recv())

    def state_step(i, carry):
        one_spread(plane_of(state_all, i), spectrum, i)
        return carry

    lax.fori_loop(0, 8, state_step, 0)

    for step in (1, 3, 2):
        position = lax.rem(column + step, 4)
        gain_arrival(position, core, gain_send, gain_recv).wait_recv()
        gain_arrival(position, core, share_send, share_recv).start()
    for step in (1, 3, 2):
        position = lax.rem(column + step, 4)
        gain_arrival(position, 1 - core, share_send, share_recv).wait_recv()

    lanes = lax.broadcasted_iota(jnp.int32, (128, 128), 1)
    mirror_low = lax.rem(4 - lanes // 32, 4) * 32 + lax.rem(32 - lax.rem(lanes, 32), 32)
    mirror_one = lanes // 32 * 32 + lax.rem(32 - lax.rem(lanes, 32), 32)

    def gain_step(h, carry):
        columns = pl.ds(pl.multiple_of(h * 128, 128), 128)
        for kind in range(2):
            block = gains[kind, :, columns]
            turned_gains[kind, h] = block.T
            flipped = jnp.take_along_axis(block, mirror_low, axis=1).T
            turned_gains[2 + kind, h] = jnp.take_along_axis(flipped, mirror_one, axis=1)
        return carry

    lax.fori_loop(0, 8, gain_step, 0)

    def load_eight(ref, rows):
        return [(ref[n, rows, :128], ref[n, rows, 128:]) for n in range(8)]

    def store_eight(ref, rows, values):
        for n, (re, im) in enumerate(values):
            ref[n, rows, :128] = re
            ref[n, rows, 128:] = im

    for residue in range(4):

        def filter_step(r, carry, residue=residue):
            rows = pl.ds(pl.multiple_of(residue * 32 + r * 8, 8), 8)
            whole = forward_eight(load_eight(spectrum, rows), residue)
            both, loss = [], []
            for n, (re, im) in enumerate(whole):
                other = (-n - (1 if residue else 0)) % 8
                left, right = turned_gains[0, n, rows, :], turned_gains[1, n, rows, :]
                left_m, right_m = turned_gains[2, other, rows, :], turned_gains[3, other, rows, :]
                even_l = (left + left_m) * 0.5
                even_r = (right + right_m) * 0.5
                even_c = (left * right + left_m * right_m) * 0.5
                even_left[n, rows, :] = even_l
                even_right[n, rows, :] = even_r
                even_loss[n, rows, :] = even_c
                both.append((even_l * re - even_r * im, even_l * im + even_r * re))
                loss.append((even_c * re, even_c * im))
            store_eight(work, rows, backward_eight(both, residue))
            store_eight(loss_work, rows, backward_eight(loss, residue))
            return carry

        lax.fori_loop(0, 4, filter_step, 0)

    def one_field(low_values):
        half = product(
            low_values,
            table[TOTAL_ROW : TOTAL_ROW + 256, :128],
            table[TOTAL_ROW : TOTAL_ROW + 256, 128:],
        ).T
        half = jnp.concatenate([half[:32], half[32:64]], axis=1)
        high, low = tables("lanes_back")
        return product(half, high[:, :128], low[:, :128])

    def back_step(i, carry):
        half = product(work[i], *tables("slots_back"))
        work[i] = product(turned(half), *tables("lanes_back"))
        loss_field[i] = one_field(loss_work[i])
        return carry

    lax.fori_loop(0, 8, back_step, 0)

    for_peers(lambda peer: from_peer(*passed_refs, peer).wait_recv())

    def forth_step(i, carry):
        weight = plane_of(passed_all, i)
        weights = jnp.concatenate([weight] * 4, axis=0)
        fields = work[i]
        crossed = jnp.concatenate([fields[:, 128:] * weights, fields[:, :128] * weights], axis=1)
        half = product(crossed, *tables("lanes"))
        work[i] = product(turned(half), *tables("slots"))
        one_spread(plane_of(state_all, i) * weight, product_spectrum, i)
        return carry

    lax.fori_loop(0, 8, forth_step, 0)

    for residue in range(4):

        def total_step(r, carry, residue=residue):
            rows = pl.ds(pl.multiple_of(residue * 32 + r * 8, 8), 8)
            pairs = forward_eight(load_eight(work, rows), residue)
            lost = forward_eight(load_eight(product_spectrum, rows), residue)
            total = []
            for n in range(8):
                (re, im), (lost_re, lost_im) = pairs[n], lost[n]
                even_l, even_r = even_left[n, rows, :], even_right[n, rows, :]
                even_c = even_loss[n, rows, :]
                total.append(
                    (
                        even_l * re + even_r * im - even_c * lost_re,
                        even_l * im - even_r * re - even_c * lost_im,
                    )
                )
            store_eight(work, rows, backward_eight(total, residue))
            return carry

        lax.fori_loop(0, 4, total_step, 0)

    def last_step(i, carry):
        value = one_field(work[i]) - plane_of(passed_all, i) * loss_field[i]
        result[pl.ds(i, 32, stride=8), :] = value
        return carry

    lax.fori_loop(0, 8, last_step, 0)

    def result_copy(peer):
        return pltpu.make_async_remote_copy(
            src_ref=result.at[pl.ds(peer * 16, 16), :],
            dst_ref=arrived.at[quad],
            send_sem=result_send.at[peer],
            recv_sem=result_recv.at[quad],
            device_id={"quad": peer},
            device_id_type=MESH,
        )

    def result_arrival(peer):
        return pltpu.make_async_remote_copy(
            src_ref=result.at[pl.ds(peer * 16, 16), :],
            dst_ref=arrived.at[peer],
            send_sem=result_send.at[peer],
            recv_sem=result_recv.at[peer],
            device_id={"quad": peer},
            device_id_type=MESH,
        )

    for_peers(lambda peer: result_copy(peer).start())
    arrived[quad] = result[pl.ds(quad * 16, 16), :]
    for_peers(lambda peer: result_arrival(peer).wait_recv())

    for j in range(2):
        rows = slice(8 * j, 8 * j + 8)
        cells = [
            arrived[cell, rows, :]
            + arrived[4 + cell, rows, :]
            + arrived[8 + cell, rows, :]
            + arrived[12 + cell, rows, :]
            for cell in range(4)
        ]
        parts = exchange_lanes(cells)
        for h in range(4):
            part = slice(8 * h, 8 * h + 8)
            out[j, part, :] = passed_own[j, part, :] + parts[h] * (1.0 / 16.0)

    halo.wait_send()
    for_peers(lambda peer: to_peer(*state_refs, peer).wait_send())
    for_peers(lambda peer: to_peer(*passed_refs, peer).wait_send())
    for_peers(lambda peer: result_copy(peer).wait_send())
    for step in (1, 3, 2):
        position = lax.rem(column + step, 4)
        gain_copy(position).wait_send()
        gain_arrival(position, core, share_send, share_recv).wait_send()


def local(adjoint_next, saved_state, gain_left, gain_right):
    share = adjoint_next.shape
    whole_field = pltpu.VMEM((8, 128, 256), jnp.float32)
    real_spectrum = pltpu.VMEM((8, 128, 128), jnp.float32)
    dma = pltpu.SemaphoreType.DMA
    in_vmem = pl.BlockSpec(memory_space=pltpu.VMEM)
    anywhere = pl.BlockSpec(memory_space=pl.ANY)
    table = jnp.asarray(make_tables())
    return pl.pallas_call(
        kernel,
        out_shape=jax.ShapeDtypeStruct(share, jnp.float32),
        in_specs=[in_vmem, in_vmem, anywhere, anywhere, anywhere],
        out_specs=in_vmem,
        scratch_shapes=[
            pltpu.VMEM((TABLE_ROWS, 256), jnp.bfloat16),
            pltpu.VMEM(share, jnp.float32),
            pltpu.VMEM(share, jnp.float32),
            pltpu.VMEM((4, 16, 128), jnp.float32),
            pltpu.VMEM((4, 16, 128), jnp.float32),
            pltpu.VMEM((256, 128), jnp.float32),
            pltpu.VMEM((256, 128), jnp.float32),
            pltpu.VMEM((256, 128), jnp.float32),
            pltpu.VMEM((16, 16, 128), jnp.float32),
            pltpu.VMEM((2, 128, 1024), jnp.float32),
            pltpu.VMEM((4, 8, 128, 128), jnp.float32),
            real_spectrum,
            real_spectrum,
            real_spectrum,
            whole_field,
            whole_field,
            whole_field,
            whole_field,
            pltpu.VMEM((8, 32, 128), jnp.float32),
            dma((3,)),
            dma((2,)),
            dma((16,)),
            dma((16,)),
            dma((16,)),
            dma((16,)),
            dma((16,)),
            dma((16,)),
            dma((4,)),
            dma((4,)),
            dma((4,)),
            dma((4,)),
        ],
        compiler_params=pltpu.CompilerParams(
            collective_id=0, has_side_effects=True, vmem_limit_bytes=40 * 1024 * 1024
        ),
        name="adjoint_step",
    )(adjoint_next, saved_state, gain_left, gain_right, table)


def solution(mesh):
    in_specs = (
        P("quad", None, "tile"),
        P("quad", None, "tile"),
        P("quad", None, None),
        P("quad", None, None),
    )
    out_specs = P("quad", None, "tile")
    return jax.shard_map(local, mesh=mesh, in_specs=in_specs, out_specs=out_specs, check_vma=False)
```

profile of v0, /device:TPU:1, one launch (start us, length us, event | category | flops | bytes accessed | tf_op | source)
XLA Modules:
  0.0 55.8 jit_solution(5901487308122506756)
XLA Ops:
  0.0 0.0 copy-start
  0.0 1.3 %copy-done = bf16[2432,256]{1,0:T(8,128)(2,1)S(1)} copy-done((bf16[2432,256]{1,0:T(8,128)(2,1)S(1)}, bf16[2432,256]{1,0:T(8,128)(2,1)}, u32[]{:S(2)}) %copy-start) | copy-done | bytes 1245208
  1.3 0.0 copy-start.1
  1.3 0.9 %copy-done.1 = f32[1,32,1024]{2,1,0:T(8,128)S(1)} copy-done((f32[1,32,1024]{2,1,0:T(8,128)S(1)}, f32[1,32,1024]{2,1,0:T(8,128)}, u32[]{:S(2)}) %copy-start.1) | copy-done | bytes 131096
  2.2 0.0 copy-start.2
  2.2 0.9 %copy-done.2 = f32[1,32,1024]{2,1,0:T(8,128)S(1)} copy-done((f32[1,32,1024]{2,1,0:T(8,128)S(1)}, f32[1,32,1024]{2,1,0:T(8,128)}, u32[]{:S(2)}) %copy-start.2) | copy-done | bytes 131096
  3.1 0.0 copy-start.3
  3.1 0.8 %copy-done.3 = f32[2,32,128]{2,1,0:T(8,128)S(1)} copy-done((f32[2,32,128]{2,1,0:T(8,128)S(1)}, f32[2,32,128]{2,1,0:T(8,128)}, u32[]{:S(2)}) %copy-start.3) | copy-done | bytes 32792
  3.9 0.0 copy-start.4
  3.9 0.8 %copy-done.4 = f32[2,32,128]{2,1,0:T(8,128)S(1)} copy-done((f32[2,32,128]{2,1,0:T(8,128)S(1)}, f32[2,32,128]{2,1,0:T(8,128)}, u32[]{:S(2)}) %copy-start.4) | copy-done | bytes 32792
  4.6 50.6 %adjoint_step.1 = f32[2,32,128]{2,1,0:T(8,128)S(1)} custom-call(f32[2,32,128]{2,1,0:T(8,128)S(1)} %copy-done.3, f32[2,32,128]{2,1,0:T(8,128)S(1)} %copy-done.4, f32[1,32,1024]{2,1,0:T(8,128)S(1)} %copy-done.1, f32[1,32,1024]{2,1,0:T(8,128)S(1)} %copy-done.2, bf16[2432,256]{1,0:T(8,128)(2,1)S(1)} %copy-done), custom_call_target="tpu_custom_call" | custom-call | tf_op jit(solution)/shard_map/adjoint_step/pallas_call | solution.py:512
  55.2 0.6 %copy.7 = f32[2,32,128]{2,1,0:T(8,128)} copy(f32[2,32,128]{2,1,0:T(8,128)S(1)} %adjoint_step.1) | data formatting | bytes 65536
Async XLA Ops:
  0.0 1.3 %copy-start = (bf16[2432,256]{1,0:T(8,128)(2,1)S(1)}, bf16[2432,256]{1,0:T(8,128)(2,1)}, u32[]{:S(2)}) copy-start(bf16[2432,256]{1,0:T(8,128)(2,1)} %constant.2.clone.table_hbm) | copy-start | bytes 3735556
  1.3 0.9 %copy-start.1 = (f32[1,32,1024]{2,1,0:T(8,128)S(1)}, f32[1,32,1024]{2,1,0:T(8,128)}, u32[]{:S(2)}) copy-start(f32[1,32,1024]{2,1,0:T(8,128)} %gain_left.1) | copy-start | bytes 393220
  2.2 0.9 %copy-start.2 = (f32[1,32,1024]{2,1,0:T(8,128)S(1)}, f32[1,32,1024]{2,1,0:T(8,128)}, u32[]{:S(2)}) copy-start(f32[1,32,1024]{2,1,0:T(8,128)} %gain_right.1) | copy-start | bytes 393220
  3.1 0.8 %copy-start.3 = (f32[2,32,128]{2,1,0:T(8,128)S(1)}, f32[2,32,128]{2,1,0:T(8,128)}, u32[]{:S(2)}) copy-start(f32[2,32,128]{2,1,0:T(8,128)} %adjoint.1) | copy-start | bytes 98308
  3.9 0.8 %copy-start.4 = (f32[2,32,128]{2,1,0:T(8,128)S(1)}, f32[2,32,128]{2,1,0:T(8,128)}, u32[]{:S(2)}) copy-start(f32[2,32,128]{2,1,0:T(8,128)} %state.1) | copy-start | bytes 98308
where the time goes:
time: 56.1 us; the launch traced here: 55.8 us
  Pallas kernels  50.6 us (90%)
  local copies, waits for them, and re-layouts  5.23 us (9%)
    pallas_call x1, Pallas kernels, local(): pl.pallas_call(kernel, out_shape=jax.ShapeDtypeStruct(share, jnp.float32)...  50.6 us
    unnamed x11, local copies, waits for them, and re-layouts  5.23 us

commit v1 on v0

--- a/solution.py
+++ b/solution.py
@@ -10,6 +10,12 @@
 
 MESH = pl.DeviceIdType.MESH
 NV = 32
+BLOCK = 8
+FARTHEST_FIRST = sorted(
+    ((over, across) for over in range(4) for across in range(4) if over or across),
+    key=lambda step: -(2 * min(step[0], 4 - step[0]) + min(step[1], 4 - step[1])),
+)
+HALF = 640
 ROOT_HALF = float(np.sqrt(0.5))
 
 
@@ -66,7 +72,7 @@
 def product(x, high, low):
     xh, xl = split(x)
     dot = functools.partial(jnp.dot, preferred_element_type=jnp.float32)
-    return dot(xh, high) + dot(xl, high) + dot(xh, low)
+    return dot(jnp.concatenate([xh, xl, xh], axis=1), jnp.concatenate([high, high, low], axis=0))
 
 
 def turned(x):
@@ -141,13 +147,15 @@
 
 
 def kernel(
-    adjoint,
-    state,
+    adjoint_hbm,
+    state_hbm,
     gain_left,
     gain_right,
     table_hbm,
     out,
     table,
+    adjoint,
+    state,
     beside,
     passed_own,
     state_sent,
@@ -156,16 +164,13 @@
     passed_all,
     result,
     arrived,
+    raw,
     gains,
-    turned_gains,
-    even_left,
-    even_right,
-    even_loss,
+    even,
     spectrum,
     product_spectrum,
     work,
     loss_work,
-    loss_field,
     local_sem,
     halo_sem,
     state_send,
@@ -178,6 +183,8 @@
     gain_recv,
     share_send,
     share_recv,
+    loss_send,
+    loss_recv,
 ):
     tile = lax.axis_index("tile")
     quad = lax.axis_index("quad")
@@ -192,12 +199,12 @@
     target_tile = jnp.where(ahead, down, up)
 
     fetch_table = pltpu.make_async_copy(table_hbm, table, local_sem.at[0])
-    fetch_left = pltpu.make_async_copy(
-        gain_left.at[0], gains.at[0, pl.ds(column * 32, 32), :], local_sem.at[1]
-    )
-    fetch_right = pltpu.make_async_copy(
-        gain_right.at[0], gains.at[1, pl.ds(column * 32, 32), :], local_sem.at[2]
-    )
+    fetch_left = pltpu.make_async_copy(gain_left.at[0], raw.at[0], local_sem.at[1])
+    fetch_right = pltpu.make_async_copy(gain_right.at[0], raw.at[1], local_sem.at[2])
+    fetch_state = pltpu.make_async_copy(state_hbm, state, local_sem.at[3])
+    fetch_adjoint = pltpu.make_async_copy(adjoint_hbm, adjoint, local_sem.at[4])
+    fetch_state.start()
+    fetch_adjoint.start()
     fetch_left.start()
     fetch_right.start()
     fetch_table.start()
@@ -213,6 +220,39 @@
     pl.semaphore_signal(barrier, inc=1, device_id={"tile": source_tile}, device_id_type=MESH)
     pl.semaphore_signal(barrier, inc=1, device_id={"tile": sibling}, device_id_type=MESH)
 
+    fetch_left.wait()
+    fetch_right.wait()
+    lane = lax.broadcasted_iota(jnp.int32, (8, 128), 1)
+    line = lax.broadcasted_iota(jnp.int32, (8, 128), 0)
+    mirror_lane = lax.rem(4 - lane // 32, 4) * 32 + lax.rem(32 - lax.rem(lane, 32), 32)
+    mirror_line = lax.rem(8 - line, 8)
+
+    def mirrored_source(kind, h, r):
+        def lines(t, n):
+            return raw[kind, 8 * n : 8 * n + 8, 128 * t : 128 * t + 128]
+
+        def column_mirrored(n):
+            return jnp.where(lane < 32, lines((8 - h) % 8, n), lines((7 - h) % 8, n))
+
+        first = column_mirrored((4 - r) % 4)
+        rest = jnp.take_along_axis(column_mirrored(3 - r), mirror_line, axis=0)
+        return jnp.where(line == 0, first, rest)
+
+    own_rows = column * 32
+    for h in range(5):
+        for r in range(4):
+            at = pl.ds(own_rows + 8 * r, 8)
+            here = slice(128 * h, 128 * h + 128)
+            left, right = (raw[kind, 8 * r : 8 * r + 8, here] for kind in range(2))
+            left_m, right_m = (
+                jnp.take_along_axis(source, mirror_lane, axis=1)
+                for source in (mirrored_source(0, h, r), mirrored_source(1, h, r))
+            )
+            gains[0, at, here] = (left + left_m) * 0.5
+            gains[1, at, here] = (right + right_m) * 0.5
+            gains[2, at, here] = (left * right + left_m * right_m) * 0.5
+
+    fetch_state.wait()
     for j in range(2):
         cells = exchange_lanes([state[j, 8 * h : 8 * h + 8, :] for h in range(4)])
         for cell in range(4):
@@ -229,6 +269,7 @@
         device_id={"tile": target_tile},
         device_id_type=MESH,
     )
+    fetch_adjoint.wait()
     halo.start()
 
     def to_peer(sent, whole, send, recv, peer):
@@ -252,25 +293,18 @@
         )
 
     def for_peers(action):
-        def body(step, carry):
-            action(lax.rem(quad + step, 16))
-            return carry
-
-        lax.fori_loop(1, 16, body, 0)
+        for over, across in FARTHEST_FIRST:
+            action(lax.rem(row + over, 4) * 4 + lax.rem(column + across, 4))
 
     state_refs = (state_sent, state_all, state_send, state_recv)
     passed_refs = (passed_sent, passed_all, passed_send, passed_recv)
-    for_peers(lambda peer: to_peer(*state_refs, peer).start())
-
-    fetch_left.wait()
-    fetch_right.wait()
-
-    def gain_copy(position):
+
+    def gain_copy(kind, send, recv, position):
         return pltpu.make_async_remote_copy(
-            src_ref=gains.at[core, pl.ds(column * 32, 32), :],
-            dst_ref=gains.at[core, pl.ds(column * 32, 32), :],
-            send_sem=gain_send.at[position],
-            recv_sem=gain_recv.at[column],
+            src_ref=gains.at[kind, pl.ds(column * 32, 32), :],
+            dst_ref=gains.at[kind, pl.ds(column * 32, 32), :],
+            send_sem=send.at[position],
+            recv_sem=recv.at[column],
             device_id={"quad": row * 4 + position},
             device_id_type=MESH,
         )
@@ -285,11 +319,12 @@
             device_id_type=MESH,
         )
 
-    for step in (1, 3, 2):
-        gain_copy(lax.rem(column + step, 4)).start()
+    beside_columns = [lax.rem(column + step, 4) for step in (2, 1, 3)]
+    for position in beside_columns:
+        gain_copy(core, gain_send, gain_recv, position).start()
+    for_peers(lambda peer: to_peer(*state_refs, peer).start())
 
     halo.wait_recv()
-    lane = lax.broadcasted_iota(jnp.int32, (8, 128), 1)
     lower = lane < 64
     odd_cell = lane // 32 % 2 == 1
     from_own = jnp.logical_xor(lower, jnp.logical_not(ahead))
@@ -314,16 +349,19 @@
             passed_sent[cell, 8 * j : 8 * j + 8, :] = cells[cell]
     passed_all[pl.ds(quad * 16, 16), :] = passed_sent[column]
     for_peers(lambda peer: to_peer(*passed_refs, peer).start())
+    for position in beside_columns:
+        gain_copy(2, loss_send, loss_recv, position).start()
 
     def tables(name):
         high, low, count = ROWS_OF[name]
         return table[high : high + count, :], table[low : low + count, :]
 
-    def one_spread(values, store, low_index):
+    def spread(values):
         high, low = tables("lanes")
         mid = product(values, high[:128], low[:128])
-        mid = jnp.concatenate([mid[:, :128], mid[:, 128:]], axis=0).T
-        store[low_index] = product(mid, *tables("spread"))
+        parts = [mid[n : n + 32] for n in range(0, values.shape[0], 32)]
+        parts = [jnp.concatenate([part[:, :128], part[:, 128:]], axis=0).T for part in parts]
+        return product(jnp.concatenate(parts, axis=0), *tables("spread"))
 
     def plane_of(ref, low_index):
         return ref[pl.ds(low_index, 32, stride=8), :]
@@ -331,34 +369,9 @@
     fetch_table.wait()
     for_peers(lambda peer: from_peer(*state_refs, peer).wait_recv())
 
-    def state_step(i, carry):
-        one_spread(plane_of(state_all, i), spectrum, i)
-        return carry
-
-    lax.fori_loop(0, 8, state_step, 0)
-
-    for step in (1, 3, 2):
-        position = lax.rem(column + step, 4)
-        gain_arrival(position, core, gain_send, gain_recv).wait_recv()
-        gain_arrival(position, core, share_send, share_recv).start()
-    for step in (1, 3, 2):
-        position = lax.rem(column + step, 4)
-        gain_arrival(position, 1 - core, share_send, share_recv).wait_recv()
-
-    lanes = lax.broadcasted_iota(jnp.int32, (128, 128), 1)
-    mirror_low = lax.rem(4 - lanes // 32, 4) * 32 + lax.rem(32 - lax.rem(lanes, 32), 32)
-    mirror_one = lanes // 32 * 32 + lax.rem(32 - lax.rem(lanes, 32), 32)
-
-    def gain_step(h, carry):
-        columns = pl.ds(pl.multiple_of(h * 128, 128), 128)
-        for kind in range(2):
-            block = gains[kind, :, columns]
-            turned_gains[kind, h] = block.T
-            flipped = jnp.take_along_axis(block, mirror_low, axis=1).T
-            turned_gains[2 + kind, h] = jnp.take_along_axis(flipped, mirror_one, axis=1)
-        return carry
-
-    lax.fori_loop(0, 8, gain_step, 0)
+    for i in range(0, 8, BLOCK):
+        planes = jnp.concatenate([plane_of(state_all, i + n) for n in range(BLOCK)], axis=0)
+        spectrum[i : i + BLOCK] = spread(planes).reshape(BLOCK, 128, 256)
 
     def load_eight(ref, rows):
         return [(ref[n, rows, :128], ref[n, rows, 128:]) for n in range(8)]
@@ -368,90 +381,123 @@
             ref[n, rows, :128] = re
             ref[n, rows, 128:] = im
 
-    for residue in range(4):
-
-        def filter_step(r, carry, residue=residue):
-            rows = pl.ds(pl.multiple_of(residue * 32 + r * 8, 8), 8)
-            whole = forward_eight(load_eight(spectrum, rows), residue)
-            both, loss = [], []
-            for n, (re, im) in enumerate(whole):
-                other = (-n - (1 if residue else 0)) % 8
-                left, right = turned_gains[0, n, rows, :], turned_gains[1, n, rows, :]
-                left_m, right_m = turned_gains[2, other, rows, :], turned_gains[3, other, rows, :]
-                even_l = (left + left_m) * 0.5
-                even_r = (right + right_m) * 0.5
-                even_c = (left * right + left_m * right_m) * 0.5
-                even_left[n, rows, :] = even_l
-                even_right[n, rows, :] = even_r
-                even_loss[n, rows, :] = even_c
-                both.append((even_l * re - even_r * im, even_l * im + even_r * re))
-                loss.append((even_c * re, even_c * im))
-            store_eight(work, rows, backward_eight(both, residue))
-            store_eight(loss_work, rows, backward_eight(loss, residue))
-            return carry
-
-        lax.fori_loop(0, 4, filter_step, 0)
-
-    def one_field(low_values):
+    def over_rows(step):
+        for residue in range(4):
+
+            def body(r, carry, residue=residue):
+                step(residue, pl.ds(pl.multiple_of(residue * 32 + r * 8, 8), 8))
+                return carry
+
+            lax.fori_loop(0, 4, body, 0)
+
+    def finish_forward(ref):
+        def step(residue, rows):
+            store_eight(ref, rows, forward_eight(load_eight(ref, rows), residue))
+
+        over_rows(step)
+
+    finish_forward(spectrum)
+
+    lanes = lax.broadcasted_iota(jnp.int32, (128, 128), 1)
+    mirror_low = lax.rem(4 - lanes // 32, 4) * 32 + lax.rem(32 - lax.rem(lanes, 32), 32)
+    mirror_one = lanes // 32 * 32 + lax.rem(32 - lax.rem(lanes, 32), 32)
+
+    def unfold(kind):
+        for h in range(5):
+            block = gains[kind, :, 128 * h : 128 * h + 128]
+            if h == 4:
+                even[kind, 4, :32, :] = block.T[:32]
+                continue
+            even[kind, h] = block.T
+            other = jnp.take_along_axis(block, mirror_low, axis=1).T
+            other = jnp.take_along_axis(other, mirror_one, axis=1)
+            even[kind, 7 - h, 32:, :] = other[32:]
+            if h:
+                even[kind, 8 - h, :32, :] = other[:32]
+
+    for position in beside_columns:
+        gain_arrival(position, core, gain_send, gain_recv).wait_recv()
+        gain_arrival(position, core, share_send, share_recv).start()
+    unfold(core)
+
+    for_peers(lambda peer: from_peer(*passed_refs, peer).wait_recv())
+    for i in range(0, 8, BLOCK):
+        planes = [plane_of(state_all, n) * plane_of(passed_all, n) for n in range(i, i + BLOCK)]
+        fields = spread(jnp.concatenate(planes, axis=0))
+        product_spectrum[i : i + BLOCK] = fields.reshape(BLOCK, 128, 256)
+    finish_forward(product_spectrum)
+
+    for position in beside_columns:
+        gain_arrival(position, 1 - core, share_send, share_recv).wait_recv()
+    unfold(1 - core)
+
+    def filter_step(residue, rows):
+        both = []
+        for n, (re, im) in enumerate(load_eight(spectrum, rows)):
+            left, right = even[0, n, rows, :], even[1, n, rows, :]
+            both.append((left * re - right * im, left * im + right * re))
+        store_eight(work, rows, backward_eight(both, residue))
+
+    over_rows(filter_step)
+
+    def summed_fields(values):
         half = product(
-            low_values,
+            values,
             table[TOTAL_ROW : TOTAL_ROW + 256, :128],
             table[TOTAL_ROW : TOTAL_ROW + 256, 128:],
-        ).T
-        half = jnp.concatenate([half[:32], half[32:64]], axis=1)
+        )
+        parts = [half[n : n + 128].T for n in range(0, values.shape[0], 128)]
+        parts = [jnp.concatenate([part[:32], part[32:64]], axis=1) for part in parts]
         high, low = tables("lanes_back")
-        return product(half, high[:, :128], low[:, :128])
-
-    def back_step(i, carry):
-        half = product(work[i], *tables("slots_back"))
-        work[i] = product(turned(half), *tables("lanes_back"))
-        loss_field[i] = one_field(loss_work[i])
-        return carry
-
-    lax.fori_loop(0, 8, back_step, 0)
-
-    for_peers(lambda peer: from_peer(*passed_refs, peer).wait_recv())
-
-    def forth_step(i, carry):
-        weight = plane_of(passed_all, i)
-        weights = jnp.concatenate([weight] * 4, axis=0)
-        fields = work[i]
-        crossed = jnp.concatenate([fields[:, 128:] * weights, fields[:, :128] * weights], axis=1)
-        half = product(crossed, *tables("lanes"))
-        work[i] = product(turned(half), *tables("slots"))
-        one_spread(plane_of(state_all, i) * weight, product_spectrum, i)
-        return carry
-
-    lax.fori_loop(0, 8, forth_step, 0)
-
-    for residue in range(4):
-
-        def total_step(r, carry, residue=residue):
-            rows = pl.ds(pl.multiple_of(residue * 32 + r * 8, 8), 8)
-            pairs = forward_eight(load_eight(work, rows), residue)
-            lost = forward_eight(load_eight(product_spectrum, rows), residue)
-            total = []
-            for n in range(8):
-                (re, im), (lost_re, lost_im) = pairs[n], lost[n]
-                even_l, even_r = even_left[n, rows, :], even_right[n, rows, :]
-                even_c = even_loss[n, rows, :]
-                total.append(
-                    (
-                        even_l * re + even_r * im - even_c * lost_re,
-                        even_l * im - even_r * re - even_c * lost_im,
-                    )
-                )
-            store_eight(work, rows, backward_eight(total, residue))
-            return carry
-
-        lax.fori_loop(0, 4, total_step, 0)
-
-    def last_step(i, carry):
-        value = one_field(work[i]) - plane_of(passed_all, i) * loss_field[i]
-        result[pl.ds(i, 32, stride=8), :] = value
-        return carry
-
-    lax.fori_loop(0, 8, last_step, 0)
+        return product(jnp.concatenate(parts, axis=0), high[:, :128], low[:, :128])
+
+    def all_turned(values):
+        parts = [turned(values[n : n + 128]) for n in range(0, values.shape[0], 128)]
+        return jnp.concatenate(parts, axis=0)
+
+    for i in range(0, 8, BLOCK):
+        half = product(work[i : i + BLOCK].reshape(BLOCK * 128, 256), *tables("slots_back"))
+        fields = product(all_turned(half), *tables("lanes_back"))
+        work[i : i + BLOCK] = fields.reshape(BLOCK, 128, 256)
+    for i in range(0, 8, BLOCK):
+        crossed = []
+        for n in range(i, i + BLOCK):
+            weights = jnp.concatenate([plane_of(passed_all, n)] * 4, axis=0)
+            fields = work[n]
+            crossed.append(
+                jnp.concatenate([fields[:, 128:] * weights, fields[:, :128] * weights], axis=1)
+            )
+        half = product(jnp.concatenate(crossed, axis=0), *tables("lanes"))
+        fields = product(all_turned(half), *tables("slots"))
+        work[i : i + BLOCK] = fields.reshape(BLOCK, 128, 256)
+    for position in beside_columns:
+        gain_arrival(position, 2, loss_send, loss_recv).wait_recv()
+    unfold(2)
+
+    def total_step(residue, rows):
+        pairs = forward_eight(load_eight(work, rows), residue)
+        lost = load_eight(product_spectrum, rows)
+        whole = load_eight(spectrum, rows)
+        total, loss = [], []
+        for n in range(8):
+            (re, im), (lost_re, lost_im) = pairs[n], lost[n]
+            left, right, both = (even[kind, n, rows, :] for kind in range(3))
+            total.append(
+                (left * re + right * im - both * lost_re, left * im - right * re - both * lost_im)
+            )
+            loss.append((both * whole[n][0], both * whole[n][1]))
+        store_eight(work, rows, backward_eight(total, residue))
+        store_eight(loss_work, rows, backward_eight(loss, residue))
+
+    over_rows(total_step)
+
+    for i in range(0, 8, BLOCK):
+        fields = summed_fields(work[i : i + BLOCK].reshape(BLOCK * 128, 256))
+        losses = summed_fields(loss_work[i : i + BLOCK].reshape(BLOCK * 128, 256))
+        for n in range(BLOCK):
+            own = slice(32 * n, 32 * n + 32)
+            value = fields[own] - plane_of(passed_all, i + n) * losses[own]
+            result[pl.ds(i + n, 32, stride=8), :] = value
 
     def result_copy(peer):
         return pltpu.make_async_remote_copy(
@@ -495,16 +541,15 @@
     for_peers(lambda peer: to_peer(*state_refs, peer).wait_send())
     for_peers(lambda peer: to_peer(*passed_refs, peer).wait_send())
     for_peers(lambda peer: result_copy(peer).wait_send())
-    for step in (1, 3, 2):
-        position = lax.rem(column + step, 4)
-        gain_copy(position).wait_send()
+    for position in beside_columns:
+        gain_copy(core, gain_send, gain_recv, position).wait_send()
+        gain_copy(2, loss_send, loss_recv, position).wait_send()
         gain_arrival(position, core, share_send, share_recv).wait_send()
 
 
 def local(adjoint_next, saved_state, gain_left, gain_right):
     share = adjoint_next.shape
     whole_field = pltpu.VMEM((8, 128, 256), jnp.float32)
-    real_spectrum = pltpu.VMEM((8, 128, 128), jnp.float32)
     dma = pltpu.SemaphoreType.DMA
     in_vmem = pl.BlockSpec(memory_space=pltpu.VMEM)
     anywhere = pl.BlockSpec(memory_space=pl.ANY)
@@ -512,10 +557,12 @@
     return pl.pallas_call(
         kernel,
         out_shape=jax.ShapeDtypeStruct(share, jnp.float32),
-        in_specs=[in_vmem, in_vmem, anywhere, anywhere, anywhere],
+        in_specs=[anywhere] * 5,
         out_specs=in_vmem,
         scratch_shapes=[
             pltpu.VMEM((TABLE_ROWS, 256), jnp.bfloat16),
+            pltpu.VMEM(share, jnp.float32),
+            pltpu.VMEM(share, jnp.float32),
             pltpu.VMEM(share, jnp.float32),
             pltpu.VMEM(share, jnp.float32),
             pltpu.VMEM((4, 16, 128), jnp.float32),
@@ -524,17 +571,14 @@
             pltpu.VMEM((256, 128), jnp.float32),
             pltpu.VMEM((256, 128), jnp.float32),
             pltpu.VMEM((16, 16, 128), jnp.float32),
-            pltpu.VMEM((2, 128, 1024), jnp.float32),
-            pltpu.VMEM((4, 8, 128, 128), jnp.float32),
-            real_spectrum,
-            real_spectrum,
-            real_spectrum,
+            pltpu.VMEM((2, NV, 1024), jnp.float32),
+            pltpu.VMEM((3, 128, HALF), jnp.float32),
+            pltpu.VMEM((3, 8, 128, 128), jnp.float32),
             whole_field,
             whole_field,
             whole_field,
             whole_field,
-            pltpu.VMEM((8, 32, 128), jnp.float32),
-            dma((3,)),
+            dma((5,)),
             dma((2,)),
             dma((16,)),
             dma((16,)),
@@ -546,9 +590,11 @@
             dma((4,)),
             dma((4,)),
             dma((4,)),
+            dma((4,)),
+            dma((4,)),
         ],
         compiler_params=pltpu.CompilerParams(
-            collective_id=0, has_side_effects=True, vmem_limit_bytes=40 * 1024 * 1024
+            collective_id=0, has_side_effects=True, vmem_limit_bytes=60 * 1024 * 1024
         ),
         name="adjoint_step",
     )(adjoint_next, saved_state, gain_left, gain_right, table)

time: 56.1 us -> 38.8 us (0.69)
  the two profiles are of different devices: /device:TPU:1 before, /device:TPU:24 now
where the time goes in v1:
time: 38.8 us; the launch traced here: 38.6 us
  Pallas kernels  37.3 us (96%)
  local copies, waits for them, and re-layouts  1.38 us (4%)
    pallas_call x1, Pallas kernels, local(): pl.pallas_call(kernel, out_shape=jax.ShapeDtypeStruct(share, jnp.float32)...  37.3 us
    unnamed x1, local copies, waits for them, and re-layouts  1.38 us

profile of v1, /device:TPU:24, one launch (start us, length us, event | category | flops | bytes accessed | tf_op | source)
XLA Modules:
  0.0 38.6 jit_solution(4987525096061328266)
XLA Ops:
  0.0 37.3 %adjoint_step.1 = f32[2,32,128]{2,1,0:T(8,128)} custom-call(f32[2,32,128]{2,1,0:T(8,128)} %adjoint_hbm.1, f32[2,32,128]{2,1,0:T(8,128)} %state_hbm.1, f32[1,32,1024]{2,1,0:T(8,128)} %gain_left.1, f32[1,32,1024]{2,1,0:T(8,128)} %gain_right.1, bf16[2432,256]{1,0:T(8,128)(2,1)} %constant.2.clone.table_hbm), custom_call_target="tpu_custom_call" | custom-call | tf_op jit(solution)/shard_map/adjoint_step/pallas_call | solution.py:557
  37.3 1.4 %copy.7 = f32[2,32,128]{2,1,0:T(8,128)} copy(f32[2,32,128]{2,1,0:T(8,128)} %adjoint_step.1) | data formatting | bytes 65536

commit v2 on v1

--- a/solution.py
+++ b/solution.py
@@ -39,28 +39,38 @@
     blocks = [
         in_real_form(lanes),
         in_real_form(slots),
-        in_real_form(np.tile(whole, (1, 4))),
         in_real_form(slots.conj() / NV),
         in_real_form(lanes.conj() / NV**2),
     ]
     rows = []
     for block in blocks:
         rows.extend(two_halves(block))
-    total = in_real_form(np.tile(whole.conj() / NV, (4, 1)))
-    total = np.concatenate([total, np.zeros((256, 64))], axis=1)
-    rows.append(np.concatenate(two_halves(total), axis=1))
+    back = whole.conj() / NV
+    for left in (
+        np.concatenate([whole.real, whole.imag], axis=0),
+        np.concatenate([back.real, -back.imag], axis=1),
+    ):
+        high, low = two_halves(left)
+        wide = np.concatenate([high, high, low], axis=1)
+        rows.append(np.pad(wide, ((0, 0), (0, 256 - wide.shape[1]))))
     return np.concatenate(rows, axis=0)
 
 
+def make_twiddles():
+    angle = -2.0 * np.pi * (np.arange(8)[:, None] * (np.arange(128)[None, :] // 32)) / NV
+    parts = np.stack([np.cos(angle), np.sin(angle)], axis=1).astype(np.float32)
+    return np.broadcast_to(parts[:, :, None, :], (8, 2, 8, 128)).reshape(128, 128).copy()
+
+
 ROWS_OF = {
-    "lanes": (0, 256, 256),
-    "slots": (512, 768, 256),
-    "spread": (1024, 1088, 64),
-    "slots_back": (1152, 1408, 256),
-    "lanes_back": (1664, 1920, 256),
+    "lanes": (0, 256),
+    "slots": (512, 768),
+    "slots_back": (1024, 1280),
+    "lanes_back": (1536, 1792),
 }
-TOTAL_ROW = 2176
-TABLE_ROWS = 2432
+LEFT_ROW = 2048
+LEFT_BACK_ROW = 2112
+TABLE_ROWS = 2144
 
 
 def split(x):
@@ -69,10 +79,20 @@
     return high, low
 
 
+def dot(a, b):
+    return jnp.dot(a, b, preferred_element_type=jnp.float32)
+
+
 def product(x, high, low):
     xh, xl = split(x)
-    dot = functools.partial(jnp.dot, preferred_element_type=jnp.float32)
-    return dot(jnp.concatenate([xh, xl, xh], axis=1), jnp.concatenate([high, high, low], axis=0))
+    return dot(
+        jnp.concatenate([xh, xl, xh], axis=1), jnp.concatenate([high, high, low], axis=0)
+    )
+
+
+def left_product(left, x):
+    xh, xl = split(x)
+    return dot(left, jnp.concatenate([xh, xl, xh], axis=0))
 
 
 def turned(x):
@@ -82,8 +102,6 @@
 def turn_by(value, factor):
     re, im = value
     fr, fi = factor
-    if abs(fi) < 1e-12 and abs(fr - 1.0) < 1e-12:
-        return value
     return (re * fr - im * fi, re * fi + im * fr)
 
 
@@ -118,17 +136,14 @@
     return [plus(e, o) for e, o in zip(even, odd)] + [minus(e, o) for e, o in zip(even, odd)]
 
 
-def twiddle(index, residue, sign):
-    angle = sign * 2.0 * np.pi * (index * residue % NV) / NV
-    return float(np.cos(angle)), float(np.sin(angle))
-
-
-def forward_eight(x, residue):
-    return eight_points([turn_by(v, twiddle(n, residue, -1)) for n, v in enumerate(x)], -1)
-
-
-def backward_eight(x, residue):
-    return [turn_by(v, twiddle(n, residue, 1)) for n, v in enumerate(eight_points(x, 1))]
+def forward_eight(x, factors):
+    turned_x = [x[0]] + [turn_by(v, f) for v, f in zip(x[1:], factors)]
+    return eight_points(turned_x, -1)
+
+
+def backward_eight(x, factors):
+    y = eight_points(x, 1)
+    return [y[0]] + [turn_by(v, (fr, -fi)) for v, (fr, fi) in zip(y[1:], factors)]
 
 
 def exchange_lanes(tiles):
@@ -152,8 +167,10 @@
     gain_left,
     gain_right,
     table_hbm,
+    twiddle_hbm,
     out,
     table,
+    twiddles,
     adjoint,
     state,
     beside,
@@ -166,11 +183,14 @@
     arrived,
     raw,
     gains,
-    even,
+    upper,
+    loss_gain,
+    loss_upper,
     spectrum,
     product_spectrum,
+    total,
+    loss,
     work,
-    loss_work,
     local_sem,
     halo_sem,
     state_send,
@@ -198,6 +218,7 @@
     source_tile = jnp.where(ahead, up, down)
     target_tile = jnp.where(ahead, down, up)
 
+    fetch_twiddles = pltpu.make_async_copy(twiddle_hbm, twiddles, local_sem.at[5])
     fetch_table = pltpu.make_async_copy(table_hbm, table, local_sem.at[0])
     fetch_left = pltpu.make_async_copy(gain_left.at[0], raw.at[0], local_sem.at[1])
     fetch_right = pltpu.make_async_copy(gain_right.at[0], raw.at[1], local_sem.at[2])
@@ -208,6 +229,7 @@
     fetch_left.start()
     fetch_right.start()
     fetch_table.start()
+    fetch_twiddles.start()
 
     barrier = pltpu.get_barrier_semaphore()
 
@@ -227,27 +249,24 @@
     mirror_lane = lax.rem(4 - lane // 32, 4) * 32 + lax.rem(32 - lax.rem(lane, 32), 32)
     mirror_line = lax.rem(8 - line, 8)
 
-    def mirrored_source(kind, h, r):
-        def lines(t, n):
-            return raw[kind, 8 * n : 8 * n + 8, 128 * t : 128 * t + 128]
-
-        def column_mirrored(n):
-            return jnp.where(lane < 32, lines((8 - h) % 8, n), lines((7 - h) % 8, n))
-
-        first = column_mirrored((4 - r) % 4)
-        rest = jnp.take_along_axis(column_mirrored(3 - r), mirror_line, axis=0)
-        return jnp.where(line == 0, first, rest)
+    def mirrored(tile_of, h, r):
+        def column(n):
+            return jnp.where(lane < 32, tile_of((8 - h) % 8, n), tile_of((7 - h) % 8, n))
+
+        rest = jnp.take_along_axis(column(3 - r), mirror_line, axis=0)
+        both = jnp.where(line == 0, column((4 - r) % 4), rest)
+        return jnp.take_along_axis(both, mirror_lane, axis=1)
+
+    def raw_tile(kind):
+        return lambda h, r: raw[kind, 8 * r : 8 * r + 8, 128 * h : 128 * h + 128]
 
     own_rows = column * 32
     for h in range(5):
         for r in range(4):
             at = pl.ds(own_rows + 8 * r, 8)
             here = slice(128 * h, 128 * h + 128)
-            left, right = (raw[kind, 8 * r : 8 * r + 8, here] for kind in range(2))
-            left_m, right_m = (
-                jnp.take_along_axis(source, mirror_lane, axis=1)
-                for source in (mirrored_source(0, h, r), mirrored_source(1, h, r))
-            )
+            left, right = raw_tile(0)(h, r), raw_tile(1)(h, r)
+            left_m, right_m = mirrored(raw_tile(0), h, r), mirrored(raw_tile(1), h, r)
             gains[0, at, here] = (left + left_m) * 0.5
             gains[1, at, here] = (right + right_m) * 0.5
             gains[2, at, here] = (left * right + left_m * right_m) * 0.5
@@ -353,25 +372,18 @@
         gain_copy(2, loss_send, loss_recv, position).start()
 
     def tables(name):
-        high, low, count = ROWS_OF[name]
-        return table[high : high + count, :], table[low : low + count, :]
-
-    def spread(values):
-        high, low = tables("lanes")
-        mid = product(values, high[:128], low[:128])
-        parts = [mid[n : n + 32] for n in range(0, values.shape[0], 32)]
-        parts = [jnp.concatenate([part[:, :128], part[:, 128:]], axis=0).T for part in parts]
-        return product(jnp.concatenate(parts, axis=0), *tables("spread"))
+        high, low = ROWS_OF[name]
+        return table[high : high + 256, :], table[low : low + 256, :]
 
     def plane_of(ref, low_index):
         return ref[pl.ds(low_index, 32, stride=8), :]
 
-    fetch_table.wait()
-    for_peers(lambda peer: from_peer(*state_refs, peer).wait_recv())
-
-    for i in range(0, 8, BLOCK):
-        planes = jnp.concatenate([plane_of(state_all, i + n) for n in range(BLOCK)], axis=0)
-        spectrum[i : i + BLOCK] = spread(planes).reshape(BLOCK, 128, 256)
+    def tile_at(n):
+        return slice(128 * n, 128 * n + 128)
+
+    def factors():
+        at = [slice(8 * n, 8 * n + 8) for n in range(16)]
+        return [(twiddles[at[2 * n], :], twiddles[at[2 * n + 1], :]) for n in range(1, 8)]
 
     def load_eight(ref, rows):
         return [(ref[n, rows, :128], ref[n, rows, 128:]) for n in range(8)]
@@ -381,123 +393,154 @@
             ref[n, rows, :128] = re
             ref[n, rows, 128:] = im
 
-    def over_rows(step):
-        for residue in range(4):
-
-            def body(r, carry, residue=residue):
-                step(residue, pl.ds(pl.multiple_of(residue * 32 + r * 8, 8), 8))
-                return carry
-
-            lax.fori_loop(0, 4, body, 0)
-
-    def finish_forward(ref):
-        def step(residue, rows):
-            store_eight(ref, rows, forward_eight(load_eight(ref, rows), residue))
-
-        over_rows(step)
-
-    finish_forward(spectrum)
-
-    lanes = lax.broadcasted_iota(jnp.int32, (128, 128), 1)
-    mirror_low = lax.rem(4 - lanes // 32, 4) * 32 + lax.rem(32 - lax.rem(lanes, 32), 32)
-    mirror_one = lanes // 32 * 32 + lax.rem(32 - lax.rem(lanes, 32), 32)
+    def eight_rows(start):
+        return pl.ds(pl.multiple_of(start, 8), 8)
+
+    def transform(planes, ref):
+        left = table[LEFT_ROW : LEFT_ROW + 64, :96]
+        mid = left_product(left, jnp.concatenate(planes, axis=1))
+        rows = [
+            jnp.concatenate([mid[:32, tile_at(n)], mid[32:, tile_at(n)]], axis=1) for n in range(8)
+        ]
+        ref[...] = product(jnp.concatenate(rows, axis=0), *tables("lanes")).reshape(8, NV, 256)
+
+        def finish(r, carry):
+            rows = eight_rows(8 * r)
+            store_eight(ref, rows, forward_eight(load_eight(ref, rows), factors()))
+            return carry
+
+        lax.fori_loop(0, 4, finish, 0)
+
+    fetch_table.wait()
+    fetch_twiddles.wait()
+    for_peers(lambda peer: from_peer(*state_refs, peer).wait_recv())
+    transform([plane_of(state_all, n) for n in range(8)], spectrum)
 
     def unfold(kind):
-        for h in range(5):
-            block = gains[kind, :, 128 * h : 128 * h + 128]
-            if h == 4:
-                even[kind, 4, :32, :] = block.T[:32]
-                continue
-            even[kind, h] = block.T
-            other = jnp.take_along_axis(block, mirror_low, axis=1).T
-            other = jnp.take_along_axis(other, mirror_one, axis=1)
-            even[kind, 7 - h, 32:, :] = other[32:]
-            if h:
-                even[kind, 8 - h, :32, :] = other[:32]
+        def body(pair, carry):
+            def tile_of(h, r):
+                return gains[kind, eight_rows(pair * 32 + 8 * r), tile_at(h)]
+
+            for h in (7, 6, 5, 4):
+                for r in range(4):
+                    values = mirrored(tile_of, h, r)
+                    if h == 4:
+                        values = jnp.where(lane < 32, tile_of(4, r), values)
+                    upper[kind, eight_rows(pair * 32 + 8 * r), tile_at(h - 4)] = values
+            return carry
+
+        lax.fori_loop(0, 4, body, 0)
 
     for position in beside_columns:
         gain_arrival(position, core, gain_send, gain_recv).wait_recv()
         gain_arrival(position, core, share_send, share_recv).start()
     unfold(core)
 
-    for_peers(lambda peer: from_peer(*passed_refs, peer).wait_recv())
-    for i in range(0, 8, BLOCK):
-        planes = [plane_of(state_all, n) * plane_of(passed_all, n) for n in range(i, i + BLOCK)]
-        fields = spread(jnp.concatenate(planes, axis=0))
-        product_spectrum[i : i + BLOCK] = fields.reshape(BLOCK, 128, 256)
-    finish_forward(product_spectrum)
+    def wait_passed():
+        for_peers(lambda peer: from_peer(*passed_refs, peer).wait_recv())
+
+    def transform_product():
+        planes = [plane_of(state_all, n) * plane_of(passed_all, n) for n in range(8)]
+        transform(planes, product_spectrum)
 
     for position in beside_columns:
         gain_arrival(position, 1 - core, share_send, share_recv).wait_recv()
     unfold(1 - core)
 
-    def filter_step(residue, rows):
+    def gain_tile(kind, rows, n):
+        return gains[kind, rows, tile_at(n)] if n < 4 else upper[kind, rows, tile_at(n - 4)]
+
+    def filter_step(r, carry):
+        rows = eight_rows(8 * r)
         both = []
-        for n, (re, im) in enumerate(load_eight(spectrum, rows)):
-            left, right = even[0, n, rows, :], even[1, n, rows, :]
+        for n, (re, im) in enumerate(load_eight(spectrum, eight_rows(8 * lax.rem(r, 4)))):
+            left, right = gain_tile(0, rows, n), gain_tile(1, rows, n)
             both.append((left * re - right * im, left * im + right * re))
-        store_eight(work, rows, backward_eight(both, residue))
-
-    over_rows(filter_step)
-
-    def summed_fields(values):
-        half = product(
-            values,
-            table[TOTAL_ROW : TOTAL_ROW + 256, :128],
-            table[TOTAL_ROW : TOTAL_ROW + 256, 128:],
-        )
-        parts = [half[n : n + 128].T for n in range(0, values.shape[0], 128)]
-        parts = [jnp.concatenate([part[:32], part[32:64]], axis=1) for part in parts]
-        high, low = tables("lanes_back")
-        return product(jnp.concatenate(parts, axis=0), high[:, :128], low[:, :128])
+        store_eight(work, rows, backward_eight(both, factors()))
+        return carry
+
+    lax.fori_loop(0, 16, filter_step, 0)
 
     def all_turned(values):
-        parts = [turned(values[n : n + 128]) for n in range(0, values.shape[0], 128)]
+        parts = [turned(values[tile_at(n)]) for n in range(values.shape[0] // 128)]
         return jnp.concatenate(parts, axis=0)
 
     for i in range(0, 8, BLOCK):
-        half = product(work[i : i + BLOCK].reshape(BLOCK * 128, 256), *tables("slots_back"))
-        fields = product(all_turned(half), *tables("lanes_back"))
+        half = product(work[i : i + BLOCK].reshape(BLOCK * 128, 256), *tables("lanes_back"))
+        fields = product(all_turned(half), *tables("slots_back"))
         work[i : i + BLOCK] = fields.reshape(BLOCK, 128, 256)
+
+    wait_passed()
     for i in range(0, 8, BLOCK):
         crossed = []
         for n in range(i, i + BLOCK):
-            weights = jnp.concatenate([plane_of(passed_all, n)] * 4, axis=0)
+            weights = jnp.concatenate([plane_of(passed_all, n)] * 4, axis=0).T
             fields = work[n]
             crossed.append(
                 jnp.concatenate([fields[:, 128:] * weights, fields[:, :128] * weights], axis=1)
             )
-        half = product(jnp.concatenate(crossed, axis=0), *tables("lanes"))
-        fields = product(all_turned(half), *tables("slots"))
+        half = product(jnp.concatenate(crossed, axis=0), *tables("slots"))
+        fields = product(all_turned(half), *tables("lanes"))
         work[i : i + BLOCK] = fields.reshape(BLOCK, 128, 256)
+    transform_product()
+
     for position in beside_columns:
         gain_arrival(position, 2, loss_send, loss_recv).wait_recv()
-    unfold(2)
-
-    def total_step(residue, rows):
-        pairs = forward_eight(load_eight(work, rows), residue)
-        lost = load_eight(product_spectrum, rows)
-        whole = load_eight(spectrum, rows)
-        total, loss = [], []
-        for n in range(8):
-            (re, im), (lost_re, lost_im) = pairs[n], lost[n]
-            left, right, both = (even[kind, n, rows, :] for kind in range(3))
-            total.append(
-                (left * re + right * im - both * lost_re, left * im - right * re - both * lost_im)
-            )
-            loss.append((both * whole[n][0], both * whole[n][1]))
-        store_eight(work, rows, backward_eight(total, residue))
-        store_eight(loss_work, rows, backward_eight(loss, residue))
-
-    over_rows(total_step)
-
-    for i in range(0, 8, BLOCK):
-        fields = summed_fields(work[i : i + BLOCK].reshape(BLOCK * 128, 256))
-        losses = summed_fields(loss_work[i : i + BLOCK].reshape(BLOCK * 128, 256))
-        for n in range(BLOCK):
-            own = slice(32 * n, 32 * n + 32)
-            value = fields[own] - plane_of(passed_all, i + n) * losses[own]
-            result[pl.ds(i + n, 32, stride=8), :] = value
+
+    def loss_tile(h, r):
+        return loss_gain[8 * r : 8 * r + 8, tile_at(h)]
+
+    for r in range(4):
+        for h in range(5):
+            starts = [32 * pair + 8 * r for pair in range(4)]
+            b = [gains[2, start : start + 8, tile_at(h)] for start in starts]
+            loss_gain[8 * r : 8 * r + 8, tile_at(h)] = (b[0] + b[1]) + (b[2] + b[3])
+    for h in (7, 6, 5, 4):
+        for r in range(4):
+            values = mirrored(loss_tile, h, r)
+            if h == 4:
+                values = jnp.where(lane < 32, loss_tile(4, r), values)
+            loss_upper[8 * r : 8 * r + 8, tile_at(h - 4)] = values
+
+    def total_step(r, carry):
+        rows = eight_rows(8 * r)
+        sums = []
+        weights = [loss_gain[rows, tile_at(n)] for n in range(4)]
+        weights += [loss_upper[rows, tile_at(n)] for n in range(4)]
+        for n, (re, im) in enumerate(load_eight(product_spectrum, rows)):
+            sums.append((-weights[n] * re, -weights[n] * im))
+        for pair in range(4):
+            at = eight_rows(32 * pair + 8 * r)
+            for n, (re, im) in enumerate(forward_eight(load_eight(work, at), factors())):
+                left, right = gain_tile(0, at, n), gain_tile(1, at, n)
+                sums[n] = (
+                    sums[n][0] + (left * re + right * im),
+                    sums[n][1] + (left * im - right * re),
+                )
+        store_eight(total, rows, backward_eight(sums, factors()))
+        lost = [
+            (weights[n] * re, weights[n] * im)
+            for n, (re, im) in enumerate(load_eight(spectrum, rows))
+        ]
+        store_eight(loss, rows, backward_eight(lost, factors()))
+        return carry
+
+    lax.fori_loop(0, 4, total_step, 0)
+
+    both = jnp.concatenate([total[...].reshape(256, 256), loss[...].reshape(256, 256)], axis=0)
+    both = product(both, *tables("lanes_back"))
+
+    def last_axis(values):
+        parts = [values[32 * n : 32 * n + 32] for n in range(8)]
+        re = jnp.concatenate([part[:, :128] for part in parts], axis=1)
+        im = jnp.concatenate([part[:, 128:] for part in parts], axis=1)
+        left = table[LEFT_BACK_ROW : LEFT_BACK_ROW + 32, :192]
+        return left_product(left, jnp.concatenate([re, im], axis=0))
+
+    gained, lost = last_axis(both[:256]), last_axis(both[256:])
+    for n in range(8):
+        value = gained[:, tile_at(n)] - plane_of(passed_all, n) * lost[:, tile_at(n)]
+        result[pl.ds(n, 32, stride=8), :] = value
 
     def result_copy(peer):
         return pltpu.make_async_remote_copy(
@@ -550,6 +593,7 @@
 def local(adjoint_next, saved_state, gain_left, gain_right):
     share = adjoint_next.shape
     whole_field = pltpu.VMEM((8, 128, 256), jnp.float32)
+    one_field = pltpu.VMEM((8, NV, 256), jnp.float32)
     dma = pltpu.SemaphoreType.DMA
     in_vmem = pl.BlockSpec(memory_space=pltpu.VMEM)
     anywhere = pl.BlockSpec(memory_space=pl.ANY)
@@ -557,10 +601,11 @@
     return pl.pallas_call(
         kernel,
         out_shape=jax.ShapeDtypeStruct(share, jnp.float32),
-        in_specs=[anywhere] * 5,
+        in_specs=[anywhere] * 6,
         out_specs=in_vmem,
         scratch_shapes=[
             pltpu.VMEM((TABLE_ROWS, 256), jnp.bfloat16),
+            pltpu.VMEM((128, 128), jnp.float32),
             pltpu.VMEM(share, jnp.float32),
             pltpu.VMEM(share, jnp.float32),
             pltpu.VMEM(share, jnp.float32),
@@ -573,12 +618,15 @@
             pltpu.VMEM((16, 16, 128), jnp.float32),
             pltpu.VMEM((2, NV, 1024), jnp.float32),
             pltpu.VMEM((3, 128, HALF), jnp.float32),
-            pltpu.VMEM((3, 8, 128, 128), jnp.float32),
+            pltpu.VMEM((2, 128, 512), jnp.float32),
+            pltpu.VMEM((NV, HALF), jnp.float32),
+            pltpu.VMEM((NV, 512), jnp.float32),
+            one_field,
+            one_field,
+            one_field,
+            one_field,
             whole_field,
-            whole_field,
-            whole_field,
-            whole_field,
-            dma((5,)),
+            dma((6,)),
             dma((2,)),
             dma((16,)),
             dma((16,)),
@@ -597,7 +645,7 @@
             collective_id=0, has_side_effects=True, vmem_limit_bytes=60 * 1024 * 1024
         ),
         name="adjoint_step",
-    )(adjoint_next, saved_state, gain_left, gain_right, table)
+    )(adjoint_next, saved_state, gain_left, gain_right, table, jnp.asarray(make_twiddles()))
 
 
 def solution(mesh):

time: 38.8 us -> 36.4 us (0.938)
  the two profiles are of different devices: /device:TPU:24 before, /device:TPU:1 now
where the time goes in v2:
time: 36.4 us; the launch traced here: 36.2 us
  Pallas kernels  34.8 us (96%)
  local copies, waits for them, and re-layouts  1.38 us (4%)
    pallas_call x1, Pallas kernels, local(): pl.pallas_call(kernel, out_shape=jax.ShapeDtypeStruct(share, jnp.float32)...  34.8 us
    unnamed x1, local copies, waits for them, and re-layouts  1.38 us

profile of v2, /device:TPU:1, one launch (start us, length us, event | category | flops | bytes accessed | tf_op | source)
XLA Modules:
  0.0 36.2 jit_solution(17613087893090332685)
XLA Ops:
  0.0 34.8 %adjoint_step.1 = f32[2,32,128]{2,1,0:T(8,128)} custom-call(f32[2,32,128]{2,1,0:T(8,128)} %adjoint_hbm.1, f32[2,32,128]{2,1,0:T(8,128)} %state_hbm.1, f32[1,32,1024]{2,1,0:T(8,128)} %gain_left.1, f32[1,32,1024]{2,1,0:T(8,128)} %gain_right.1, bf16[2144,256]{1,0:T(8,128)(2,1)} %constant.4.clone.table_hbm, f32[128,128]{1,0:T(8,128)} %constant.5.clone.twiddle_hbm), custom_call_target="tpu_custom_call" | custom-call | tf_op jit(solution)/shard_map/adjoint_step/pallas_call | solution.py:601
  34.8 1.4 %copy.8 = f32[2,32,128]{2,1,0:T(8,128)} copy(f32[2,32,128]{2,1,0:T(8,128)} %adjoint_step.1) | data formatting | bytes 65536

commit v3 on v2

--- a/solution.py
+++ b/solution.py
@@ -218,6 +218,14 @@
     source_tile = jnp.where(ahead, up, down)
     target_tile = jnp.where(ahead, down, up)
 
+    barrier = pltpu.get_barrier_semaphore()
+
+    for over, across in FARTHEST_FIRST:
+        peer = lax.rem(row + over, 4) * 4 + lax.rem(column + across, 4)
+        pl.semaphore_signal(barrier, inc=1, device_id={"quad": peer}, device_id_type=MESH)
+    pl.semaphore_signal(barrier, inc=1, device_id={"tile": source_tile}, device_id_type=MESH)
+    pl.semaphore_signal(barrier, inc=1, device_id={"tile": sibling}, device_id_type=MESH)
+
     fetch_twiddles = pltpu.make_async_copy(twiddle_hbm, twiddles, local_sem.at[5])
     fetch_table = pltpu.make_async_copy(table_hbm, table, local_sem.at[0])
     fetch_left = pltpu.make_async_copy(gain_left.at[0], raw.at[0], local_sem.at[1])
@@ -230,17 +238,6 @@
     fetch_right.start()
     fetch_table.start()
     fetch_twiddles.start()
-
-    barrier = pltpu.get_barrier_semaphore()
-
-    def greet(step, carry):
-        peer = lax.rem(quad + step, 16)
-        pl.semaphore_signal(barrier, inc=1, device_id={"quad": peer}, device_id_type=MESH)
-        return carry
-
-    lax.fori_loop(1, 16, greet, 0)
-    pl.semaphore_signal(barrier, inc=1, device_id={"tile": source_tile}, device_id_type=MESH)
-    pl.semaphore_signal(barrier, inc=1, device_id={"tile": sibling}, device_id_type=MESH)
 
     fetch_left.wait()
     fetch_right.wait()
@@ -368,8 +365,6 @@
             passed_sent[cell, 8 * j : 8 * j + 8, :] = cells[cell]
     passed_all[pl.ds(quad * 16, 16), :] = passed_sent[column]
     for_peers(lambda peer: to_peer(*passed_refs, peer).start())
-    for position in beside_columns:
-        gain_copy(2, loss_send, loss_recv, position).start()
 
     def tables(name):
         high, low = ROWS_OF[name]
@@ -432,6 +427,9 @@
         lax.fori_loop(0, 4, body, 0)
 
     for position in beside_columns:
+        gain_copy(2, loss_send, loss_recv, position).start()
+
+    for position in beside_columns:
         gain_arrival(position, core, gain_send, gain_recv).wait_recv()
         gain_arrival(position, core, share_send, share_recv).start()
     unfold(core)
@@ -442,6 +440,9 @@
     def transform_product():
         planes = [plane_of(state_all, n) * plane_of(passed_all, n) for n in range(8)]
         transform(planes, product_spectrum)
+
+    wait_passed()
+    transform_product()
 
     for position in beside_columns:
         gain_arrival(position, 1 - core, share_send, share_recv).wait_recv()
@@ -470,7 +471,6 @@
         fields = product(all_turned(half), *tables("slots_back"))
         work[i : i + BLOCK] = fields.reshape(BLOCK, 128, 256)
 
-    wait_passed()
     for i in range(0, 8, BLOCK):
         crossed = []
         for n in range(i, i + BLOCK):
@@ -482,7 +482,6 @@
         half = product(jnp.concatenate(crossed, axis=0), *tables("slots"))
         fields = product(all_turned(half), *tables("lanes"))
         work[i : i + BLOCK] = fields.reshape(BLOCK, 128, 256)
-    transform_product()
 
     for position in beside_columns:
         gain_arrival(position, 2, loss_send, loss_recv).wait_recv()

time: 36.4 us -> 34.9 us (0.959)
  the two profiles are of different devices: /device:TPU:1 before, /device:TPU:32 now
where the time goes in v3:
time: 34.9 us; the launch traced here: 34.7 us
  Pallas kernels  33.3 us (95%)
  local copies, waits for them, and re-layouts  1.38 us (4%)
    pallas_call x1, Pallas kernels, local(): pl.pallas_call(kernel, out_shape=jax.ShapeDtypeStruct(share, jnp.float32)...  33.3 us
    unnamed x1, local copies, waits for them, and re-layouts  1.38 us

profile of v3, /device:TPU:32, one launch (start us, length us, event | category | flops | bytes accessed | tf_op | source)
XLA Modules:
  0.0 34.7 jit_solution(12896240514496072938)
XLA Ops:
  0.0 33.3 %adjoint_step.1 = f32[2,32,128]{2,1,0:T(8,128)} custom-call(f32[2,32,128]{2,1,0:T(8,128)} %adjoint_hbm.1, f32[2,32,128]{2,1,0:T(8,128)} %state_hbm.1, f32[1,32,1024]{2,1,0:T(8,128)} %gain_left.1, f32[1,32,1024]{2,1,0:T(8,128)} %gain_right.1, bf16[2144,256]{1,0:T(8,128)(2,1)} %constant.4.clone.table_hbm, f32[128,128]{1,0:T(8,128)} %constant.5.clone.twiddle_hbm), custom_call_target="tpu_custom_call" | custom-call | tf_op jit(solution)/shard_map/adjoint_step/pallas_call | solution.py:600
  33.3 1.4 %copy.8 = f32[2,32,128]{2,1,0:T(8,128)} copy(f32[2,32,128]{2,1,0:T(8,128)} %adjoint_step.1) | data formatting | bytes 65536

commit v4 on v3

--- a/solution.py
+++ b/solution.py
@@ -12,7 +12,7 @@
 NV = 32
 BLOCK = 8
 FARTHEST_FIRST = sorted(
-    ((over, across) for over in range(4) for across in range(4) if over or across),
+    ((over, across) for over in range(4) for across in range(4)),
     key=lambda step: -(2 * min(step[0], 4 - step[0]) + min(step[1], 4 - step[1])),
 )
 HALF = 640
@@ -205,6 +205,8 @@
     share_recv,
     loss_send,
     loss_recv,
+    near_here,
+    far_here,
 ):
     tile = lax.axis_index("tile")
     quad = lax.axis_index("quad")
@@ -213,18 +215,34 @@
     row = quad // 4
     core = lax.rem(tile, 2)
     sibling = tile + 1 - 2 * core
+    partner_tile = lax.rem(tile + tiles // 2, tiles)
     ahead = quad >= 8
     up, down = lax.rem(tile + 1, tiles), lax.rem(tile + tiles - 1, tiles)
     source_tile = jnp.where(ahead, up, down)
     target_tile = jnp.where(ahead, down, up)
 
     barrier = pltpu.get_barrier_semaphore()
-
+    even_tile = tile - core
+    far_listener = partner_tile - core + 1
     for over, across in FARTHEST_FIRST:
         peer = lax.rem(row + over, 4) * 4 + lax.rem(column + across, 4)
-        pl.semaphore_signal(barrier, inc=1, device_id={"quad": peer}, device_id_type=MESH)
-    pl.semaphore_signal(barrier, inc=1, device_id={"tile": source_tile}, device_id_type=MESH)
-    pl.semaphore_signal(barrier, inc=1, device_id={"tile": sibling}, device_id_type=MESH)
+        pl.semaphore_signal(
+            barrier, inc=1, device_id={"tile": far_listener, "quad": peer}, device_id_type=MESH
+        )
+    for step in (2, 1, 3):
+        peer = row * 4 + lax.rem(column + step, 4)
+        pl.semaphore_signal(
+            barrier, inc=1, device_id={"tile": even_tile, "quad": peer}, device_id_type=MESH
+        )
+    near_source = source_tile - lax.rem(source_tile, 2)
+
+    @pl.when(near_source != tile)
+    def _():
+        pl.semaphore_signal(barrier, inc=1, device_id={"tile": near_source}, device_id_type=MESH)
+
+    @pl.when(core == 1)
+    def _():
+        pl.semaphore_signal(barrier, inc=1, device_id={"tile": sibling}, device_id_type=MESH)
 
     fetch_twiddles = pltpu.make_async_copy(twiddle_hbm, twiddles, local_sem.at[5])
     fetch_table = pltpu.make_async_copy(table_hbm, table, local_sem.at[0])
@@ -273,9 +291,15 @@
         cells = exchange_lanes([state[j, 8 * h : 8 * h + 8, :] for h in range(4)])
         for cell in range(4):
             state_sent[cell, 8 * j : 8 * j + 8, :] = cells[cell]
-    state_all[pl.ds(quad * 16, 16), :] = state_sent[column]
-
-    pl.semaphore_wait(barrier, 17)
+
+    @pl.when(core == 0)
+    def _():
+        pl.semaphore_wait(barrier, jnp.where(ahead, 8, 9))
+        pl.semaphore_signal(near_here, inc=1, device_id={"tile": sibling}, device_id_type=MESH)
+
+    @pl.when(core == 1)
+    def _():
+        pl.semaphore_wait(near_here, 1)
 
     halo = pltpu.make_async_remote_copy(
         src_ref=adjoint,
@@ -294,7 +318,7 @@
             dst_ref=whole.at[pl.ds(quad * 16, 16), :],
             send_sem=send.at[peer],
             recv_sem=recv.at[quad],
-            device_id={"quad": peer},
+            device_id={"tile": partner_tile, "quad": peer},
             device_id_type=MESH,
         )
 
@@ -304,7 +328,7 @@
             dst_ref=whole.at[pl.ds(peer * 16, 16), :],
             send_sem=send.at[peer],
             recv_sem=recv.at[peer],
-            device_id={"quad": peer},
+            device_id={"tile": partner_tile, "quad": peer},
             device_id_type=MESH,
         )
 
@@ -338,6 +362,16 @@
     beside_columns = [lax.rem(column + step, 4) for step in (2, 1, 3)]
     for position in beside_columns:
         gain_copy(core, gain_send, gain_recv, position).start()
+
+    @pl.when(core == 1)
+    def _():
+        pl.semaphore_wait(barrier, 32)
+        pl.semaphore_signal(far_here, inc=1, device_id={"tile": sibling}, device_id_type=MESH)
+
+    @pl.when(core == 0)
+    def _():
+        pl.semaphore_wait(far_here, 1)
+
     for_peers(lambda peer: to_peer(*state_refs, peer).start())
 
     halo.wait_recv()
@@ -363,7 +397,6 @@
         cells = exchange_lanes([passed_own[j, 8 * h : 8 * h + 8, :] for h in range(4)])
         for cell in range(4):
             passed_sent[cell, 8 * j : 8 * j + 8, :] = cells[cell]
-    passed_all[pl.ds(quad * 16, 16), :] = passed_sent[column]
     for_peers(lambda peer: to_peer(*passed_refs, peer).start())
 
     def tables(name):
@@ -547,7 +580,7 @@
             dst_ref=arrived.at[quad],
             send_sem=result_send.at[peer],
             recv_sem=result_recv.at[quad],
-            device_id={"quad": peer},
+            device_id={"tile": partner_tile, "quad": peer},
             device_id_type=MESH,
         )
 
@@ -557,12 +590,11 @@
             dst_ref=arrived.at[peer],
             send_sem=result_send.at[peer],
             recv_sem=result_recv.at[peer],
-            device_id={"quad": peer},
+            device_id={"tile": partner_tile, "quad": peer},
             device_id_type=MESH,
         )
 
     for_peers(lambda peer: result_copy(peer).start())
-    arrived[quad] = result[pl.ds(quad * 16, 16), :]
     for_peers(lambda peer: result_arrival(peer).wait_recv())
 
     for j in range(2):
@@ -639,6 +671,8 @@
             dma((4,)),
             dma((4,)),
             dma((4,)),
+            pltpu.SemaphoreType.REGULAR,
+            pltpu.SemaphoreType.REGULAR,
         ],
         compiler_params=pltpu.CompilerParams(
             collective_id=0, has_side_effects=True, vmem_limit_bytes=60 * 1024 * 1024

time: 34.9 us -> 34.2 us (0.980)
  the two profiles are of different devices: /device:TPU:32 before, /device:TPU:1 now
where the time goes in v4:
time: 34.2 us; the launch traced here: 34 us
  Pallas kernels  32.6 us (95%)
  local copies, waits for them, and re-layouts  1.38 us (4%)
    pallas_call x1, Pallas kernels, local(): pl.pallas_call(kernel, out_shape=jax.ShapeDtypeStruct(share, jnp.float32)...  32.6 us
    unnamed x1, local copies, waits for them, and re-layouts  1.38 us

profile of v4, /device:TPU:1, one launch (start us, length us, event | category | flops | bytes accessed | tf_op | source)
XLA Modules:
  0.0 34.0 jit_solution(14449287360822112619)
XLA Ops:
  0.0 32.6 %adjoint_step.1 = f32[2,32,128]{2,1,0:T(8,128)} custom-call(f32[2,32,128]{2,1,0:T(8,128)} %adjoint_hbm.1, f32[2,32,128]{2,1,0:T(8,128)} %state_hbm.1, f32[1,32,1024]{2,1,0:T(8,128)} %gain_left.1, f32[1,32,1024]{2,1,0:T(8,128)} %gain_right.1, bf16[2144,256]{1,0:T(8,128)(2,1)} %constant.4.clone.table_hbm, f32[128,128]{1,0:T(8,128)} %constant.5.clone.twiddle_hbm), custom_call_target="tpu_custom_call" | custom-call | tf_op jit(solution)/shard_map/adjoint_step/pallas_call | solution.py:632
  32.6 1.4 %copy.8 = f32[2,32,128]{2,1,0:T(8,128)} copy(f32[2,32,128]{2,1,0:T(8,128)} %adjoint_step.1) | data formatting | bytes 65536

commit v5 on v4

--- a/solution.py
+++ b/solution.py
@@ -316,19 +316,19 @@
         return pltpu.make_async_remote_copy(
             src_ref=sent.at[lax.rem(peer, 4)],
             dst_ref=whole.at[pl.ds(quad * 16, 16), :],
-            send_sem=send.at[peer],
-            recv_sem=recv.at[quad],
+            send_sem=send,
+            recv_sem=recv,
             device_id={"tile": partner_tile, "quad": peer},
             device_id_type=MESH,
         )
 
-    def from_peer(sent, whole, send, recv, peer):
+    def all_of(whole, send, recv):
         return pltpu.make_async_remote_copy(
-            src_ref=sent.at[0],
-            dst_ref=whole.at[pl.ds(peer * 16, 16), :],
-            send_sem=send.at[peer],
-            recv_sem=recv.at[peer],
-            device_id={"tile": partner_tile, "quad": peer},
+            src_ref=whole,
+            dst_ref=whole,
+            send_sem=send,
+            recv_sem=recv,
+            device_id={"tile": partner_tile},
             device_id_type=MESH,
         )
 
@@ -439,11 +439,6 @@
 
         lax.fori_loop(0, 4, finish, 0)
 
-    fetch_table.wait()
-    fetch_twiddles.wait()
-    for_peers(lambda peer: from_peer(*state_refs, peer).wait_recv())
-    transform([plane_of(state_all, n) for n in range(8)], spectrum)
-
     def unfold(kind):
         def body(pair, carry):
             def tile_of(h, r):
@@ -460,15 +455,20 @@
         lax.fori_loop(0, 4, body, 0)
 
     for position in beside_columns:
-        gain_copy(2, loss_send, loss_recv, position).start()
-
-    for position in beside_columns:
         gain_arrival(position, core, gain_send, gain_recv).wait_recv()
         gain_arrival(position, core, share_send, share_recv).start()
+    for position in beside_columns:
+        gain_copy(2, loss_send, loss_recv, position).start()
     unfold(core)
 
+    fetch_table.wait()
+    fetch_twiddles.wait()
+    all_of(*state_refs[1:]).wait_recv()
+    transform([plane_of(state_all, n) for n in range(8)], spectrum)
+
+
     def wait_passed():
-        for_peers(lambda peer: from_peer(*passed_refs, peer).wait_recv())
+        all_of(*passed_refs[1:]).wait_recv()
 
     def transform_product():
         planes = [plane_of(state_all, n) * plane_of(passed_all, n) for n in range(8)]
@@ -577,33 +577,32 @@
     def result_copy(peer):
         return pltpu.make_async_remote_copy(
             src_ref=result.at[pl.ds(peer * 16, 16), :],
-            dst_ref=arrived.at[quad],
-            send_sem=result_send.at[peer],
-            recv_sem=result_recv.at[quad],
+            dst_ref=arrived.at[pl.ds(quad * 16, 16), :],
+            send_sem=result_send,
+            recv_sem=result_recv,
             device_id={"tile": partner_tile, "quad": peer},
             device_id_type=MESH,
         )
 
-    def result_arrival(peer):
-        return pltpu.make_async_remote_copy(
-            src_ref=result.at[pl.ds(peer * 16, 16), :],
-            dst_ref=arrived.at[peer],
-            send_sem=result_send.at[peer],
-            recv_sem=result_recv.at[peer],
-            device_id={"tile": partner_tile, "quad": peer},
-            device_id_type=MESH,
-        )
-
     for_peers(lambda peer: result_copy(peer).start())
-    for_peers(lambda peer: result_arrival(peer).wait_recv())
+
+    halo.wait_send()
+    all_of(*state_refs[1:]).wait_send()
+    all_of(*passed_refs[1:]).wait_send()
+    for position in beside_columns:
+        gain_copy(core, gain_send, gain_recv, position).wait_send()
+        gain_copy(2, loss_send, loss_recv, position).wait_send()
+        gain_arrival(position, core, share_send, share_recv).wait_send()
+
+    all_of(arrived, result_send, result_recv).wait_recv()
+
+    def arrived_at(source, j):
+        return arrived[16 * source + 8 * j : 16 * source + 8 * j + 8, :]
 
     for j in range(2):
-        rows = slice(8 * j, 8 * j + 8)
         cells = [
-            arrived[cell, rows, :]
-            + arrived[4 + cell, rows, :]
-            + arrived[8 + cell, rows, :]
-            + arrived[12 + cell, rows, :]
+            (arrived_at(cell, j) + arrived_at(4 + cell, j))
+            + (arrived_at(8 + cell, j) + arrived_at(12 + cell, j))
             for cell in range(4)
         ]
         parts = exchange_lanes(cells)
@@ -611,14 +610,7 @@
             part = slice(8 * h, 8 * h + 8)
             out[j, part, :] = passed_own[j, part, :] + parts[h] * (1.0 / 16.0)
 
-    halo.wait_send()
-    for_peers(lambda peer: to_peer(*state_refs, peer).wait_send())
-    for_peers(lambda peer: to_peer(*passed_refs, peer).wait_send())
-    for_peers(lambda peer: result_copy(peer).wait_send())
-    for position in beside_columns:
-        gain_copy(core, gain_send, gain_recv, position).wait_send()
-        gain_copy(2, loss_send, loss_recv, position).wait_send()
-        gain_arrival(position, core, share_send, share_recv).wait_send()
+    all_of(arrived, result_send, result_recv).wait_send()
 
 
 def local(adjoint_next, saved_state, gain_left, gain_right):
@@ -646,7 +638,7 @@
             pltpu.VMEM((256, 128), jnp.float32),
             pltpu.VMEM((256, 128), jnp.float32),
             pltpu.VMEM((256, 128), jnp.float32),
-            pltpu.VMEM((16, 16, 128), jnp.float32),
+            pltpu.VMEM((256, 128), jnp.float32),
             pltpu.VMEM((2, NV, 1024), jnp.float32),
             pltpu.VMEM((3, 128, HALF), jnp.float32),
             pltpu.VMEM((2, 128, 512), jnp.float32),
@@ -659,12 +651,12 @@
             whole_field,
             dma((6,)),
             dma((2,)),
-            dma((16,)),
-            dma((16,)),
-            dma((16,)),
-            dma((16,)),
-            dma((16,)),
-            dma((16,)),
+            dma,
+            dma,
+            dma,
+            dma,
+            dma,
+            dma,
             dma((4,)),
             dma((4,)),
             dma((4,)),

time: 34.2 us -> 32.5 us (0.950)
  Pallas kernels: 32.6 us -> 30.6 us
    pallas_call x1, Pallas kernels: 32.6 us -> 30.6 us  [local(): pl.pallas_call(kernel, out_shape=jax.ShapeDtypeStruct(share, jnp.float32)...]
where the time goes in v5:
time: 32.5 us; the launch traced here: 32 us
  Pallas kernels  30.6 us (94%)
  local copies, waits for them, and re-layouts  1.38 us (4%)
    pallas_call x1, Pallas kernels, local(): pl.pallas_call(kernel, out_shape=jax.ShapeDtypeStruct(share, jnp.float32)...  30.6 us
    unnamed x1, local copies, waits for them, and re-layouts  1.38 us

profile of v5, /device:TPU:1, one launch (start us, length us, event | category | flops | bytes accessed | tf_op | source)
XLA Modules:
  0.0 32.0 jit_solution(3097597670164668542)
XLA Ops:
  0.0 30.6 %adjoint_step.1 = f32[2,32,128]{2,1,0:T(8,128)} custom-call(f32[2,32,128]{2,1,0:T(8,128)} %adjoint_hbm.1, f32[2,32,128]{2,1,0:T(8,128)} %state_hbm.1, f32[1,32,1024]{2,1,0:T(8,128)} %gain_left.1, f32[1,32,1024]{2,1,0:T(8,128)} %gain_right.1, bf16[2144,256]{1,0:T(8,128)(2,1)} %constant.4.clone.table_hbm, f32[128,128]{1,0:T(8,128)} %constant.5.clone.twiddle_hbm), custom_call_target="tpu_custom_call" | custom-call | tf_op jit(solution)/shard_map/adjoint_step/pallas_call | solution.py:624
  30.7 1.4 %copy.8 = f32[2,32,128]{2,1,0:T(8,128)} copy(f32[2,32,128]{2,1,0:T(8,128)} %adjoint_step.1) | data formatting | bytes 65536

commit v6 on v5

--- a/solution.py
+++ b/solution.py
@@ -10,7 +10,7 @@
 
 MESH = pl.DeviceIdType.MESH
 NV = 32
-BLOCK = 8
+BLOCK = 2
 FARTHEST_FIRST = sorted(
     ((over, across) for over in range(4) for across in range(4)),
     key=lambda step: -(2 * min(step[0], 4 - step[0]) + min(step[1], 4 - step[1])),
@@ -224,11 +224,6 @@
     barrier = pltpu.get_barrier_semaphore()
     even_tile = tile - core
     far_listener = partner_tile - core + 1
-    for over, across in FARTHEST_FIRST:
-        peer = lax.rem(row + over, 4) * 4 + lax.rem(column + across, 4)
-        pl.semaphore_signal(
-            barrier, inc=1, device_id={"tile": far_listener, "quad": peer}, device_id_type=MESH
-        )
     for step in (2, 1, 3):
         peer = row * 4 + lax.rem(column + step, 4)
         pl.semaphore_signal(
@@ -243,6 +238,12 @@
     @pl.when(core == 1)
     def _():
         pl.semaphore_signal(barrier, inc=1, device_id={"tile": sibling}, device_id_type=MESH)
+
+    for over, across in FARTHEST_FIRST:
+        peer = lax.rem(row + over, 4) * 4 + lax.rem(column + across, 4)
+        pl.semaphore_signal(
+            barrier, inc=1, device_id={"tile": far_listener, "quad": peer}, device_id_type=MESH
+        )
 
     fetch_twiddles = pltpu.make_async_copy(twiddle_hbm, twiddles, local_sem.at[5])
     fetch_table = pltpu.make_async_copy(table_hbm, table, local_sem.at[0])
@@ -276,15 +277,23 @@
         return lambda h, r: raw[kind, 8 * r : 8 * r + 8, 128 * h : 128 * h + 128]
 
     own_rows = column * 32
-    for h in range(5):
-        for r in range(4):
-            at = pl.ds(own_rows + 8 * r, 8)
-            here = slice(128 * h, 128 * h + 128)
-            left, right = raw_tile(0)(h, r), raw_tile(1)(h, r)
-            left_m, right_m = mirrored(raw_tile(0), h, r), mirrored(raw_tile(1), h, r)
-            gains[0, at, here] = (left + left_m) * 0.5
-            gains[1, at, here] = (right + right_m) * 0.5
-            gains[2, at, here] = (left * right + left_m * right_m) * 0.5
+
+    def fold(kind):
+        for h in range(5):
+            for r in range(4):
+                at, here = pl.ds(own_rows + 8 * r, 8), slice(128 * h, 128 * h + 128)
+                value = raw_tile(kind)(h, r) + mirrored(raw_tile(kind), h, r)
+                gains[kind, at, here] = value * 0.5
+
+    def fold_loss():
+        for h in range(5):
+            for r in range(4):
+                at, here = pl.ds(own_rows + 8 * r, 8), slice(128 * h, 128 * h + 128)
+                direct = raw_tile(0)(h, r) * raw_tile(1)(h, r)
+                other = mirrored(raw_tile(0), h, r) * mirrored(raw_tile(1), h, r)
+                gains[2, at, here] = (direct + other) * 0.5
+
+    fold(core)
 
     fetch_state.wait()
     for j in range(2):
@@ -398,6 +407,8 @@
         for cell in range(4):
             passed_sent[cell, 8 * j : 8 * j + 8, :] = cells[cell]
     for_peers(lambda peer: to_peer(*passed_refs, peer).start())
+    fold(1 - core)
+    fold_loss()
 
     def tables(name):
         high, low = ROWS_OF[name]

time: 32.5 us -> 32 us (0.985)
  no operation moved by 1% of the time
where the time goes in v6:
time: 32 us; the launch traced here: 31.8 us
  Pallas kernels  30.4 us (95%)
  local copies, waits for them, and re-layouts  1.38 us (4%)
    pallas_call x1, Pallas kernels, local(): pl.pallas_call(kernel, out_shape=jax.ShapeDtypeStruct(share, jnp.float32)...  30.4 us
    unnamed x1, local copies, waits for them, and re-layouts  1.38 us

profile of v6, /device:TPU:1, one launch (start us, length us, event | category | flops | bytes accessed | tf_op | source)
XLA Modules:
  0.0 31.8 jit_solution(18130671913135235008)
XLA Ops:
  0.0 30.4 %adjoint_step.1 = f32[2,32,128]{2,1,0:T(8,128)} custom-call(f32[2,32,128]{2,1,0:T(8,128)} %adjoint_hbm.1, f32[2,32,128]{2,1,0:T(8,128)} %state_hbm.1, f32[1,32,1024]{2,1,0:T(8,128)} %gain_left.1, f32[1,32,1024]{2,1,0:T(8,128)} %gain_right.1, bf16[2144,256]{1,0:T(8,128)(2,1)} %constant.4.clone.table_hbm, f32[128,128]{1,0:T(8,128)} %constant.5.clone.twiddle_hbm), custom_call_target="tpu_custom_call" | custom-call | tf_op jit(solution)/shard_map/adjoint_step/pallas_call | solution.py:635
  30.4 1.4 %copy.8 = f32[2,32,128]{2,1,0:T(8,128)} copy(f32[2,32,128]{2,1,0:T(8,128)} %adjoint_step.1) | data formatting | bytes 65536
